TPU v7x, 32 devices: a whole 2x2x4 slice. The times are simulated.
32 devices in a mesh: dp: 8 (over y, x, core), ctx: 4 (over z).
Axes of the slice: x: 2, y: 2, z: 4, core: 2. Of those that a mesh axis runs over, the one named last changes fastest.
Arguments:
- tokens: bfloat16 [1024, 16, 768], P('ctx', 'dp'), may hold values from -6 to 6
- lengths: int32 [16], P('dp'), may hold values from 256 to 1024, as said below
- teacher: bfloat16 [1024, 16, 768], P('ctx', 'dp'), may hold values from -12 to 12
- query_weight: bfloat16 [768, 768], P(('dp', 'ctx')), may hold values from -0.3125 to 0.3125
- query_bias: bfloat16 [768], P(('dp', 'ctx')), may hold values from -1.1953125 to 1.1953125
- key_weight: bfloat16 [768, 768], P(('dp', 'ctx')), may hold values from -0.21875 to 0.21875
- value_weight: bfloat16 [768, 768], P(('dp', 'ctx')), may hold values from -0.21875 to 0.21875
- value_bias: bfloat16 [768], P(('dp', 'ctx')), may hold values from -1.1953125 to 1.1953125
- out_weight: bfloat16 [768, 768], P(('dp', 'ctx')), may hold values from -0.875 to 0.875
- out_bias: bfloat16 [768], P(('dp', 'ctx')), may hold values from -1.1953125 to 1.1953125
- first_gain: bfloat16 [768], P(('dp', 'ctx')), may hold values from 0.5 to 1.5
- first_shift: bfloat16 [768], P(('dp', 'ctx')), may hold values from -1.1953125 to 1.1953125
- up_weight: bfloat16 [768, 3072], P(('dp', 'ctx')), may hold values from -0.21875 to 0.21875
- up_bias: bfloat16 [3072], P(('dp', 'ctx')), may hold values from -1.1953125 to 1.1953125
- down_weight: bfloat16 [3072, 768], P(('dp', 'ctx')), may hold values from -0.109375 to 0.109375
- down_bias: bfloat16 [768], P(('dp', 'ctx')), may hold values from -1.1953125 to 1.1953125
- second_gain: bfloat16 [768], P(('dp', 'ctx')), may hold values from 0.5 to 1.5
- second_shift: bfloat16 [768], P(('dp', 'ctx')), may hold values from -1.1953125 to 1.1953125
Outputs:
- layer_out: bfloat16 [1024, 16, 768], P('ctx', 'dp')
- loss: float32 [], replicated
- grad_tokens: bfloat16 [1024, 16, 768], P('ctx', 'dp')
- grad_query_weight: float32 [768, 768], P(('dp', 'ctx'))
- grad_query_bias: float32 [768], P(('dp', 'ctx'))
- grad_key_weight: float32 [768, 768], P(('dp', 'ctx'))
- grad_value_weight: float32 [768, 768], P(('dp', 'ctx'))
- grad_value_bias: float32 [768], P(('dp', 'ctx'))
- grad_out_weight: float32 [768, 768], P(('dp', 'ctx'))
- grad_out_bias: float32 [768], P(('dp', 'ctx'))
- grad_first_gain: float32 [768], P(('dp', 'ctx'))
- grad_first_shift: float32 [768], P(('dp', 'ctx'))
- grad_up_weight: float32 [768, 3072], P(('dp', 'ctx'))
- grad_up_bias: float32 [3072], P(('dp', 'ctx'))
- grad_down_weight: float32 [3072, 768], P(('dp', 'ctx'))
- grad_down_bias: float32 [768], P(('dp', 'ctx'))
- grad_second_gain: float32 [768], P(('dp', 'ctx'))
- grad_second_shift: float32 [768], P(('dp', 'ctx'))
Inputs may be any that keep to these rules, and one draw needn't show every extreme that they name: lengths[s] is the number of valid leading slots of sequence s; later slots are padding; some sequence has 1024 valid slots in every draw.
All inputs are finite; a program needn't handle non-finite values.
Results may differ from a plain program's by a relative error of at most 0.03.
Values may be sent and summed in bfloat16 or wider, within the bound.
No kernel may reach another device: no remote copies, remote signals or barrier semaphores. Data moves between devices by JAX's collectives and lax.ppermute only.
A program may use at most 192 MiB of HBM per device.

v0:
```python
import jax
import jax.numpy as jnp
from jax import lax
from jax.sharding import PartitionSpec as P

H = 12
HD = 64


EPSILON = 1e-12
MASKED = -1e30


def normalize(values, gain, shift):
    centre = values - jnp.mean(values, axis=-1, keepdims=True)
    spread = jnp.mean(centre * centre, axis=-1, keepdims=True)
    return centre * lax.rsqrt(spread + EPSILON) * gain + shift


def activate(values):
    return jax.nn.gelu(values, approximate=True)


def product(left, right):
    return jnp.dot(left, right, preferred_element_type=jnp.float32)


def product_rows(left, right):
    return lax.dot_general(
        left, right, (((0,), (0,)), ((), ())), preferred_element_type=jnp.float32
    )


def product_back(left, right):
    return lax.dot_general(
        left, right, (((1,), (1,)), ((), ())), preferred_element_type=jnp.float32
    )


def column_sum(values):
    return jnp.sum(values.astype(jnp.float32), axis=0)


def attend(query, keyed, valued, lengths):
    width, seqs = (keyed.shape[0], keyed.shape[1])
    scale = HD ** (-0.5)
    init = (
        jnp.full((width, seqs, H), MASKED, jnp.float32),
        jnp.zeros((width, seqs, H), jnp.float32),
        jnp.zeros((width, seqs, H, HD), jnp.float32),
    )
    pieces = (
        lax.all_gather(keyed, "ctx", axis=0, tiled=True),
        lax.all_gather(valued, "ctx", axis=0, tiled=True),
    )
    count = pieces[0].shape[0] // width
    key_blocks = pieces[0].reshape(count, width, seqs, H, HD)
    value_blocks = pieces[1].reshape(count, width, seqs, H, HD)

    def attend_step(state, block):
        top, total, accum = state
        key_block, value_block, offset = block
        scores = (
            jnp.einsum("cshd,kshd->cshk", query, key_block, preferred_element_type=jnp.float32)
            * scale
        )
        place = offset * width + jnp.arange(width, dtype=jnp.int32)
        valid = place[None, :] < lengths[:, None]
        scores = jnp.where(valid[None, :, None, :], scores, MASKED)
        new_top = jnp.maximum(top, jnp.max(scores, axis=-1))
        factor = jnp.exp(top - new_top)
        probs = jnp.exp(scores - new_top[..., None])
        total = total * factor + jnp.sum(probs, axis=-1)
        accum = accum * factor[..., None] + jnp.einsum(
            "cshk,kshd->cshd",
            probs.astype(jnp.bfloat16),
            value_block,
            preferred_element_type=jnp.float32,
        )
        return ((new_top, total, accum), None)

    state, _ = lax.scan(
        attend_step, init, (key_blocks, value_blocks, jnp.arange(count, dtype=jnp.int32))
    )
    top, total, accum = state
    return (accum / total[..., None], top + jnp.log(total))


def query_grads(query, d_mixed, keyed, valued, lse, delta, lengths):
    width, seqs = (keyed.shape[0], keyed.shape[1])
    scale = HD ** (-0.5)
    init = jnp.zeros((width, seqs, H, HD), jnp.float32)
    pieces = (
        lax.all_gather(keyed, "ctx", axis=0, tiled=True),
        lax.all_gather(valued, "ctx", axis=0, tiled=True),
    )
    count = pieces[0].shape[0] // width
    key_blocks = pieces[0].reshape(count, width, seqs, H, HD)
    value_blocks = pieces[1].reshape(count, width, seqs, H, HD)

    def query_step(grad, block):
        key_block, value_block, offset = block
        scores = (
            jnp.einsum("cshd,kshd->cshk", query, key_block, preferred_element_type=jnp.float32)
            * scale
        )
        place = offset * width + jnp.arange(width, dtype=jnp.int32)
        valid = place[None, :] < lengths[:, None]
        scores = jnp.where(valid[None, :, None, :], scores, MASKED)
        probs = jnp.exp(scores - lse[..., None])
        d_probs = jnp.einsum(
            "cshd,kshd->cshk", d_mixed, value_block, preferred_element_type=jnp.float32
        )
        d_scores = (probs * (d_probs - delta[..., None])).astype(jnp.bfloat16)
        grad = (
            grad
            + jnp.einsum("cshk,kshd->cshd", d_scores, key_block, preferred_element_type=jnp.float32)
            * scale
        )
        return (grad, None)

    grad, _ = lax.scan(
        query_step, init, (key_blocks, value_blocks, jnp.arange(count, dtype=jnp.int32))
    )
    return grad


def key_grads(query, d_mixed, keyed, valued, lse, delta, lengths, place):
    width, seqs = (keyed.shape[0], keyed.shape[1])
    scale = HD ** (-0.5)
    lse_all, delta_all = (
        lax.all_gather(lse, "ctx", axis=0, tiled=True),
        lax.all_gather(delta, "ctx", axis=0, tiled=True),
    )
    valid = place[None, :] < lengths[:, None]
    zeros = jnp.zeros((width, seqs, H, HD), jnp.float32)
    pieces = (
        lax.all_gather(query, "ctx", axis=0, tiled=True),
        lax.all_gather(d_mixed, "ctx", axis=0, tiled=True),
    )
    count = pieces[0].shape[0] // width
    query_blocks = pieces[0].reshape(count, width, seqs, H, HD)
    grad_blocks = pieces[1].reshape(count, width, seqs, H, HD)

    def key_step(state, block):
        d_key, d_value = state
        query_block, grad_block, offset = block
        first_row = offset * width
        lse_block = lax.dynamic_slice_in_dim(lse_all, first_row, width, 0)
        delta_block = lax.dynamic_slice_in_dim(delta_all, first_row, width, 0)
        scores = (
            jnp.einsum("qshd,kshd->qshk", query_block, keyed, preferred_element_type=jnp.float32)
            * scale
        )
        scores = jnp.where(valid[None, :, None, :], scores, MASKED)
        probs = jnp.exp(scores - lse_block[..., None])
        d_probs = jnp.einsum(
            "qshd,kshd->qshk", grad_block, valued, preferred_element_type=jnp.float32
        )
        d_scores = (probs * (d_probs - delta_block[..., None])).astype(jnp.bfloat16)
        d_value = d_value + jnp.einsum(
            "qshk,qshd->kshd",
            probs.astype(jnp.bfloat16),
            grad_block,
            preferred_element_type=jnp.float32,
        )
        d_key = (
            d_key
            + jnp.einsum(
                "qshk,qshd->kshd", d_scores, query_block, preferred_element_type=jnp.float32
            )
            * scale
        )
        return ((d_key, d_value), None)

    state, _ = lax.scan(
        key_step, (zeros, zeros), (query_blocks, grad_blocks, jnp.arange(count, dtype=jnp.int32))
    )
    return state


def forward_layer(hidden, params, lengths):
    (
        query_weight,
        query_bias,
        key_weight,
        value_weight,
        value_bias,
        out_weight,
        out_bias,
        first_gain,
        first_shift,
        up_weight,
        up_bias,
        down_weight,
        down_bias,
        second_gain,
        second_shift,
    ) = params
    width, seqs, model = hidden.shape
    rows = width * seqs
    split = (width, seqs, H, HD)
    flat = hidden.reshape(rows, model)
    flat_low = flat.astype(jnp.bfloat16)
    query = (product(flat_low, query_weight) + query_bias.astype(jnp.float32)).astype(jnp.bfloat16)
    keyed = product(flat_low, key_weight).astype(jnp.bfloat16)
    valued = (product(flat_low, value_weight) + value_bias.astype(jnp.float32)).astype(jnp.bfloat16)
    mixed, lse = attend(query.reshape(split), keyed.reshape(split), valued.reshape(split), lengths)
    mixed_low = mixed.reshape(rows, model).astype(jnp.bfloat16)
    joined = flat + product(mixed_low, out_weight) + out_bias.astype(jnp.float32)
    first = normalize(joined, first_gain.astype(jnp.float32), first_shift.astype(jnp.float32))
    first_low = first.astype(jnp.bfloat16)
    inner = product(first_low, up_weight) + up_bias.astype(jnp.float32)
    act_low = activate(inner).astype(jnp.bfloat16)
    summed = first + product(act_low, down_weight) + down_bias.astype(jnp.float32)
    result = normalize(summed, second_gain.astype(jnp.float32), second_shift.astype(jnp.float32))
    saved = (
        flat_low,
        query,
        keyed,
        valued,
        mixed,
        lse,
        mixed_low,
        joined,
        first_low,
        inner,
        act_low,
        summed,
    )
    return (result.reshape(width, seqs, model), saved)


def backward_layer(grad_out, saved, params, lengths, place):
    (
        query_weight,
        query_bias,
        key_weight,
        value_weight,
        value_bias,
        out_weight,
        out_bias,
        first_gain,
        first_shift,
        up_weight,
        up_bias,
        down_weight,
        down_bias,
        second_gain,
        second_shift,
    ) = params
    (
        flat_low,
        query,
        keyed,
        valued,
        mixed,
        lse,
        mixed_low,
        joined,
        first_low,
        inner,
        act_low,
        summed,
    ) = saved
    width, seqs = (lse.shape[0], lse.shape[1])
    rows, model = flat_low.shape
    split = (width, seqs, H, HD)
    _, second_back = jax.vjp(
        normalize, summed, second_gain.astype(jnp.float32), second_shift.astype(jnp.float32)
    )
    d_summed, d_second_gain, d_second_shift = second_back(grad_out.reshape(rows, model))
    d_down = d_summed.astype(jnp.bfloat16)
    d_down_bias = column_sum(d_down)
    d_down_weight = product_rows(act_low, d_down)
    d_act = product_back(d_down, down_weight)
    _, act_back = jax.vjp(activate, inner)
    d_inner = act_back(d_act)[0].astype(jnp.bfloat16)
    d_up_bias = column_sum(d_inner)
    d_up_weight = product_rows(first_low, d_inner)
    d_first = d_summed + product_back(d_inner, up_weight)
    _, first_back = jax.vjp(
        normalize, joined, first_gain.astype(jnp.float32), first_shift.astype(jnp.float32)
    )
    d_joined, d_first_gain, d_first_shift = first_back(d_first)
    d_branch = d_joined.astype(jnp.bfloat16)
    d_out_bias = column_sum(d_branch)
    d_out_weight = product_rows(mixed_low, d_branch)
    d_mixed = product_back(d_branch, out_weight).astype(jnp.bfloat16).reshape(split)
    delta = jnp.sum(d_mixed.astype(jnp.float32) * mixed, axis=-1)
    query_heads = query.reshape(split)
    key_heads = keyed.reshape(split)
    value_heads = valued.reshape(split)
    d_query = query_grads(query_heads, d_mixed, key_heads, value_heads, lse, delta, lengths)
    d_key, d_value = key_grads(
        query_heads, d_mixed, key_heads, value_heads, lse, delta, lengths, place
    )
    d_query = d_query.reshape(rows, model).astype(jnp.bfloat16)
    d_key = d_key.reshape(rows, model).astype(jnp.bfloat16)
    d_value = d_value.reshape(rows, model).astype(jnp.bfloat16)
    d_hidden = (
        d_joined
        + product_back(d_query, query_weight)
        + product_back(d_key, key_weight)
        + product_back(d_value, value_weight)
    )
    grads = (
        product_rows(flat_low, d_query),
        column_sum(d_query),
        product_rows(flat_low, d_key),
        product_rows(flat_low, d_value),
        column_sum(d_value),
        d_out_weight,
        d_out_bias,
        d_first_gain,
        d_first_shift,
        d_up_weight,
        d_up_bias,
        d_down_weight,
        d_down_bias,
        d_second_gain,
        d_second_shift,
    )
    return (grads, d_hidden.reshape(width, seqs, model))


def local(
    tokens,
    lengths,
    teacher,
    query_weight,
    query_bias,
    key_weight,
    value_weight,
    value_bias,
    out_weight,
    out_bias,
    first_gain,
    first_shift,
    up_weight,
    up_bias,
    down_weight,
    down_bias,
    second_gain,
    second_shift,
):
    shards = (
        query_weight,
        query_bias,
        key_weight,
        value_weight,
        value_bias,
        out_weight,
        out_bias,
        first_gain,
        first_shift,
        up_weight,
        up_bias,
        down_weight,
        down_bias,
        second_gain,
        second_shift,
    )
    params = (
        lax.all_gather(shards[0], ("dp", "ctx"), axis=0, tiled=True),
        lax.all_gather(shards[1], ("dp", "ctx"), axis=0, tiled=True),
        lax.all_gather(shards[2], ("dp", "ctx"), axis=0, tiled=True),
        lax.all_gather(shards[3], ("dp", "ctx"), axis=0, tiled=True),
        lax.all_gather(shards[4], ("dp", "ctx"), axis=0, tiled=True),
        lax.all_gather(shards[5], ("dp", "ctx"), axis=0, tiled=True),
        lax.all_gather(shards[6], ("dp", "ctx"), axis=0, tiled=True),
        lax.all_gather(shards[7], ("dp", "ctx"), axis=0, tiled=True),
        lax.all_gather(shards[8], ("dp", "ctx"), axis=0, tiled=True),
        lax.all_gather(shards[9], ("dp", "ctx"), axis=0, tiled=True),
        lax.all_gather(shards[10], ("dp", "ctx"), axis=0, tiled=True),
        lax.all_gather(shards[11], ("dp", "ctx"), axis=0, tiled=True),
        lax.all_gather(shards[12], ("dp", "ctx"), axis=0, tiled=True),
        lax.all_gather(shards[13], ("dp", "ctx"), axis=0, tiled=True),
        lax.all_gather(shards[14], ("dp", "ctx"), axis=0, tiled=True),
    )
    width, seqs, model = tokens.shape
    place = lax.axis_index("ctx") * width + jnp.arange(width, dtype=jnp.int32)
    live = (place[:, None] < lengths[None, :]).astype(jnp.float32)
    middle, first_saved = forward_layer(tokens.astype(jnp.float32), params, lengths)
    result, second_saved = forward_layer(middle, params, lengths)
    diff = (result - teacher.astype(jnp.float32)) * live[:, :, None]
    error_sum, count = lax.psum((jnp.sum(diff * diff), jnp.sum(live)), ("dp", "ctx"))
    loss = error_sum / (count * model)
    back_params = (
        lax.all_gather(shards[0], ("dp", "ctx"), axis=0, tiled=True),
        lax.all_gather(shards[1], ("dp", "ctx"), axis=0, tiled=True),
        lax.all_gather(shards[2], ("dp", "ctx"), axis=0, tiled=True),
        lax.all_gather(shards[3], ("dp", "ctx"), axis=0, tiled=True),
        lax.all_gather(shards[4], ("dp", "ctx"), axis=0, tiled=True),
        lax.all_gather(shards[5], ("dp", "ctx"), axis=0, tiled=True),
        lax.all_gather(shards[6], ("dp", "ctx"), axis=0, tiled=True),
        lax.all_gather(shards[7], ("dp", "ctx"), axis=0, tiled=True),
        lax.all_gather(shards[8], ("dp", "ctx"), axis=0, tiled=True),
        lax.all_gather(shards[9], ("dp", "ctx"), axis=0, tiled=True),
        lax.all_gather(shards[10], ("dp", "ctx"), axis=0, tiled=True),
        lax.all_gather(shards[11], ("dp", "ctx"), axis=0, tiled=True),
        lax.all_gather(shards[12], ("dp", "ctx"), axis=0, tiled=True),
        lax.all_gather(shards[13], ("dp", "ctx"), axis=0, tiled=True),
        lax.all_gather(shards[14], ("dp", "ctx"), axis=0, tiled=True),
    )
    grads_second, d_middle = backward_layer(diff, second_saved, back_params, lengths, place)
    grads_first, d_start = backward_layer(d_middle, first_saved, back_params, lengths, place)
    total = jax.tree.map(jnp.add, grads_second, grads_first)
    owned = lax.psum_scatter(total, ("dp", "ctx"), scatter_dimension=0, tiled=True)
    return (result.astype(jnp.bfloat16), loss, d_start.astype(jnp.bfloat16)) + tuple(owned)


def solution(mesh):
    in_specs = (
        P("ctx", "dp", None),
        P("dp"),
        P("ctx", "dp", None),
        P(("dp", "ctx"), None),
        P(("dp", "ctx")),
        P(("dp", "ctx"), None),
        P(("dp", "ctx"), None),
        P(("dp", "ctx")),
        P(("dp", "ctx"), None),
        P(("dp", "ctx")),
        P(("dp", "ctx")),
        P(("dp", "ctx")),
        P(("dp", "ctx"), None),
        P(("dp", "ctx")),
        P(("dp", "ctx"), None),
        P(("dp", "ctx")),
        P(("dp", "ctx")),
        P(("dp", "ctx")),
    )
    out_specs = (
        P("ctx", "dp", None),
        P(),
        P("ctx", "dp", None),
        P(("dp", "ctx"), None),
        P(("dp", "ctx")),
        P(("dp", "ctx"), None),
        P(("dp", "ctx"), None),
        P(("dp", "ctx")),
        P(("dp", "ctx"), None),
        P(("dp", "ctx")),
        P(("dp", "ctx")),
        P(("dp", "ctx")),
        P(("dp", "ctx"), None),
        P(("dp", "ctx")),
        P(("dp", "ctx"), None),
        P(("dp", "ctx")),
        P(("dp", "ctx")),
        P(("dp", "ctx")),
    )
    return jax.shard_map(local, mesh=mesh, in_specs=in_specs, out_specs=out_specs, check_vma=False)
```

profile of v0, /device:TPU:1, one launch (start us, length us, event | category | flops | bytes accessed | tf_op | source)
XLA Modules:
  0.0 1775.8 jit_solution(14162295049002392182)
XLA Ops:
  11.7 55.5 %all-gather.15.cloned.1.call-done = bf16[768,768]{1,0:T(8,128)(2,1)} async-done(((bf16[24,768]{1,0:T(8,128)(2,1)}), bf16[768,768]{1,0:T(8,128)(2,1)}) %all-gather.15.cloned.1.call-update) | async-done | bytes 1179664 | tf_op jit(solution)/shard_map/all_gather | solution.py:367
  77.4 39.4 %all-reduce.19 = (bf16[768]{0:T(1024)(128)(2,1)S(1)}, bf16[768]{0:T(1024)(128)(2,1)S(1)}, bf16[768]{0:T(1024)(128)(2,1)S(1)}, bf16[768]{0:T(1024)(128)(2,1)S(1)}...) all-reduce(bf16[768]{0:T(1024)(128)(2,1)S(1)} %dynamic-update-slice, ...), channel_id=1, replica_groups=mesh['dp'=8,'ctx'=4] {'dp','ctx'}, use_global_device_ids=true, to_apply=%add | all-reduce | flops 9216 | bytes 36864
  134.0 45.2 %all-gather.19.cloned.1.call-done = bf16[768,768]{1,0:T(8,128)(2,1)} async-done(((bf16[24,768]{1,0:T(8,128)(2,1)}), bf16[768,768]{1,0:T(8,128)(2,1)}) %all-gather.19.cloned.1.call-update) | async-done | bytes 1179664 | tf_op jit(solution)/shard_map/all_gather | solution.py:365
  186.0 55.6 %all-gather.17.cloned.1.call-done = bf16[1024,2,12,64]{0,3,2,1:T(8,128)(2,1)} async-done(((bf16[256,2,12,64]{0,3,2,1:T(8,128)(2,1)}), bf16[1024,2,12,64]{0,3,2,1:T(8,128)(2,1)}) %all-gather.17.cloned.1.call-update) | async-done | bytes 3145744 | tf_op jit(solution)/shard_map/all_gather | solution.py:53
  245.7 59.0 %all-gather.23.cloned.1.call-done = bf16[1024,2,12,64]{0,3,2,1:T(8,128)(2,1)} async-done(((bf16[256,2,12,64]{0,3,2,1:T(8,128)(2,1)}), bf16[1024,2,12,64]{0,3,2,1:T(8,128)(2,1)}) %all-gather.23.cloned.1.call-update) | async-done | bytes 3145744 | tf_op jit(solution)/shard_map/all_gather | solution.py:54
  308.6 56.4 %while.78 = (s32[]{:T(128)}, f32[256,2,12]{0,2,1:T(8,128)S(1)}, f32[256,2,12]{0,2,1:T(8,128)S(1)}, f32[256,2,12,64]{0,3,2,1:T(8,128)S(1)}, s32[4]{0:T(128)S(1)},...) while((s32[]{:T(128)}, f32[256,2,12]{0,2,1:T(8,128)S(1)}, ...), condition=%wide.region_3.4_spmd.clone, body=%wide.region_0.3_spmd.clone.sunk | while | flops 421165824 | bytes 49942736 | solution.py:82
  377.5 49.3 %all-gather.27.cloned.1.call-done = bf16[768,3072]{1,0:T(8,128)(2,1)} async-done(((bf16[24,3072]{1,0:T(8,128)(2,1)}), bf16[768,3072]{1,0:T(8,128)(2,1)}) %all-gather.27.cloned.1.call-update) | async-done | bytes 4718608 | tf_op jit(solution)/shard_map/all_gather | solution.py:374
  433.8 57.7 %all-gather.29.cloned.1.call-done = bf16[3072,768]{1,0:T(8,128)(2,1)} async-done(((bf16[96,768]{1,0:T(8,128)(2,1)}), bf16[3072,768]{1,0:T(8,128)(2,1)}) %all-gather.29.cloned.1.call-update) | async-done | bytes 4718608 | tf_op jit(solution)/shard_map/all_gather | solution.py:376
  524.2 43.5 %all-gather.31.cloned.1.call-done = bf16[1024,2,12,64]{0,3,2,1:T(8,128)(2,1)} async-done(((bf16[256,2,12,64]{0,3,2,1:T(8,128)(2,1)}), bf16[1024,2,12,64]{0,3,2,1:T(8,128)(2,1)}) %all-gather.31.cloned.1.call-update) | async-done | bytes 3145744 | tf_op jit(solution)/shard_map/all_gather | solution.py:53
  571.6 59.1 %all-gather.33.cloned.1.call-done = bf16[1024,2,12,64]{0,3,2,1:T(8,128)(2,1)} async-done(((bf16[256,2,12,64]{0,3,2,1:T(8,128)(2,1)}), bf16[1024,2,12,64]{0,3,2,1:T(8,128)(2,1)}) %all-gather.33.cloned.1.call-update) | async-done | bytes 3145744 | tf_op jit(solution)/shard_map/all_gather | solution.py:54
  634.8 56.8 %while.79 = (s32[]{:T(128)}, f32[256,2,12]{0,2,1:T(8,128)S(1)}, f32[256,2,12]{0,2,1:T(8,128)S(1)}, f32[256,2,12,64]{0,3,2,1:T(8,128)S(1)}, s32[4]{0:T(128)S(1)},...) while((s32[]{:T(128)}, f32[256,2,12]{0,2,1:T(8,128)S(1)}, ...), condition=%wide.region_11.12_spmd.clone, body=%wide.region_8.11_spmd.clone.sunk | while | flops 421165824 | bytes 49942736 | solution.py:82
  736.1 10.3 convert_reduce_fusion.1
  771.8 22.8 %all_gather.113 = f32[1024,2,12]{0,2,1:T(8,128)S(1)} all-gather(f32[256,2,12]{0,2,1:T(8,128)S(1)} %log_add_fusion.1), channel_id=1, replica_groups=mesh['dp'=8,'ctx'=4] {'ctx'}, dimensions={0}, use_global_device_ids=true | all-gather | bytes 122880 | tf_op jit(solution)/shard_map/all_gather | solution.py:132
  794.6 54.4 %while.80 = (s32[]{:T(128)}, f32[256,2,12,64]{0,3,2,1:T(8,128)}, bf16[4,256,2,12,64]{1,4,3,2,0:T(8,128)(2,1)}, s32[4]{0:T(128)S(1)}, s32[2]{0:T(128)S(1)}, /*ind...) while((s32[]{:T(128)}, f32[256,2,12,64]{0,3,2,1:T(8,128)}, ...), condition=%wide.region_26.27_spmd.clone, body=%wide.region_25.26_spmd.clone.sunk | while | flops 614597376 | bytes 19714740 | solution.py:122
  855.2 15.1 all_gather.115
  885.4 67.7 %while.81 = (s32[]{:T(128)}, f32[256,2,12,64]{0,3,2,1:T(8,128)}, f32[256,2,12,64]{0,3,2,1:T(8,128)S(1)}, bf16[4,256,2,12,64]{1,4,3,2,0:T(8,128)(2,1)}, bf16[256,...) while((s32[]{:T(128)}, f32[256,2,12,64]{0,3,2,1:T(8,128)}, ...), condition=%wide.region_28.29_spmd.clone, body=%wide.region_27.28_spmd.clone.sunk | while | flops 823001600 | bytes 30109944 | solution.py:176
  1000.3 54.9 %while.82 = (s32[]{:T(128)}, f32[256,2,12,64]{0,3,2,1:T(8,128)}, bf16[4,256,2,12,64]{1,4,3,2,0:T(8,128)(2,1)}, s32[4]{0:T(128)S(1)}, s32[2]{0:T(128)S(1)}, /*ind...) while((s32[]{:T(128)}, f32[256,2,12,64]{0,3,2,1:T(8,128)}, ...), condition=%wide.region_35.36_spmd.clone, body=%wide.region_34.35_spmd.clone.sunk | while | flops 614597376 | bytes 35443464 | solution.py:122
  1071.2 16.5 all_gather.117
  1108.0 69.2 %while.83 = (s32[]{:T(128)}, f32[256,2,12,64]{0,3,2,1:T(8,128)}, f32[256,2,12,64]{0,3,2,1:T(8,128)S(1)}, bf16[4,256,2,12,64]{1,4,3,2,0:T(8,128)(2,1)}, bf16[256,...) while((s32[]{:T(128)}, f32[256,2,12,64]{0,3,2,1:T(8,128)}, ...), condition=%wide.region_37.38_spmd.clone, body=%wide.region_36.37_spmd.clone.sunk | while | flops 823001600 | bytes 30109944 | solution.py:176
  1236.6 45.8 %all-reduce.18 = (f32[]{:T(128)}, f32[]{:T(128)}, f32[768]{0:T(1024)S(1)}, f32[768]{0:T(1024)S(1)}, f32[768]{0:T(1024)S(1)}, /*index=5*/f32[768]{0:T(1024)S(1)},...) all-reduce(f32[]{:T(128)} %get-tuple-element.798, ...), channel_id=1, replica_groups=mesh['dp'=8,'ctx'=4] {'dp','ctx'}, use_global_device_ids=true, to_apply=%region_17.18 | all-reduce | flops 9218 | bytes 73744 | tf_op jit(solution)/shard_map/psum | solution.py:387
  1293.4 86.8 %reduce-scatter.9.cloned.1.call-done = f32[24,768]{1,0:T(8,128)} async-done(((f32[768,768]{1,0:T(8,128)}), f32[24,768]{1,0:T(8,128)}) %reduce-scatter.9.cloned.1.call-update) | async-done | bytes 73744 | tf_op jit(solution)/shard_map/reduce_scatter | solution.py:409
  1380.2 104.4 %reduce-scatter.11.cloned.1.call-done = f32[24,768]{1,0:T(8,128)} async-done(((f32[768,768]{1,0:T(8,128)}), f32[24,768]{1,0:T(8,128)}) %reduce-scatter.11.cloned.1.call-update) | async-done | bytes 73744 | tf_op jit(solution)/shard_map/reduce_scatter | solution.py:409
  1484.6 141.5 %reduce-scatter.15.cloned.1.call-done = f32[24,3072]{1,0:T(8,128)} async-done(((f32[768,3072]{1,0:T(8,128)}), f32[24,3072]{1,0:T(8,128)}) %reduce-scatter.15.cloned.1.call-update) | async-done | bytes 294928 | tf_op jit(solution)/shard_map/reduce_scatter | solution.py:409
  1626.1 141.5 %reduce-scatter.17.cloned.1.call-done = f32[96,768]{1,0:T(8,128)} async-done(((f32[3072,768]{1,0:T(8,128)}), f32[96,768]{1,0:T(8,128)}) %reduce-scatter.17.cloned.1.call-update) | async-done | bytes 294928 | tf_op jit(solution)/shard_map/reduce_scatter | solution.py:409
  (732 shorter events, 690.4 us)
Async XLA Ops:
  7.2 60.1 %all-gather.15.cloned.1.call-start = ((), (), s32[]{:S(2)}) async-start(), calls=%async_computation.6 | async-start | bytes 1216512 | tf_op jit(solution)/shard_map/all_gather | solution.py:367
  7.9 115.3 %all-gather.21.cloned.1.call-start = ((), (), s32[]{:S(2)}) async-start(), calls=%async_computation.9 | async-start | bytes 1216512 | tf_op jit(solution)/shard_map/all_gather | solution.py:368
  8.7 170.5 %all-gather.19.cloned.1.call-start = ((), (), s32[]{:S(2)}) async-start(), calls=%async_computation.8 | async-start | bytes 1216512 | tf_op jit(solution)/shard_map/all_gather | solution.py:365
  9.4 232.2 %all-gather.17.cloned.1.call-start = ((), (), s32[]{:S(2)}) async-start(), calls=%async_computation.7 | async-start | bytes 3932160 | tf_op jit(solution)/shard_map/all_gather | solution.py:53
  11.7 363.0 %copy-start.21 = (bf16[512,768]{1,0:T(8,128)(2,1)}, bf16[512,768]{1,0:T(8,128)(2,1)S(1)}, u32[]{:S(2)}) copy-start(bf16[512,768]{1,0:T(8,128)(2,1)S(1)} %reshape.449) | copy-start | bytes 2359300
  75.2 229.4 %all-gather.23.cloned.1.call-start = ((), (), s32[]{:S(2)}) async-start(), calls=%async_computation.10 | async-start | bytes 3932160 | tf_op jit(solution)/shard_map/all_gather | solution.py:54
  131.1 243.6 %all-gather.25.cloned.1.call-start = ((), (), s32[]{:S(2)}) async-start(), calls=%async_computation.11 | async-start | bytes 1216512 | tf_op jit(solution)/shard_map/all_gather | solution.py:370
  131.7 295.1 %all-gather.27.cloned.1.call-start = ((), (), s32[]{:S(2)}) async-start(), calls=%async_computation.12 | async-start | bytes 4866048 | tf_op jit(solution)/shard_map/all_gather | solution.py:374
  132.5 359.1 %all-gather.29.cloned.1.call-start = ((), (), s32[]{:S(2)}) async-start(), calls=%async_computation.13 | async-start | bytes 4866048 | tf_op jit(solution)/shard_map/all_gather | solution.py:376
  133.2 434.5 %all-gather.31.cloned.1.call-start = ((), (), s32[]{:S(2)}) async-start(), calls=%async_computation.14 | async-start | bytes 3932160 | tf_op jit(solution)/shard_map/all_gather | solution.py:53
  133.8 357.7 %copy-start.118 = (f32[768]{0:T(1024)}, f32[768]{0:T(1024)S(1)}, u32[]{:S(2)}) copy-start(f32[768]{0:T(1024)S(1)} %convert_element_type.253) | copy-start | bytes 9220
  133.9 357.7 %copy-start.59 = (f32[768]{0:T(1024)}, f32[768]{0:T(1024)S(1)}, u32[]{:S(2)}) copy-start(f32[768]{0:T(1024)S(1)} %convert_element_type.249) | copy-start | bytes 9220
  133.9 365.8 %copy-start.69 = (f32[768]{0:T(1024)}, f32[768]{0:T(1024)S(1)}, u32[]{:S(2)}) copy-start(f32[768]{0:T(1024)S(1)} %convert_element_type.255) | copy-start | bytes 9220
  507.8 123.0 %all-gather.33.cloned.1.call-start = ((), (), s32[]{:S(2)}) async-start(), calls=%async_computation.15 | async-start | bytes 3932160 | tf_op jit(solution)/shard_map/all_gather | solution.py:54
  515.7 335.6 %all-gather.35.cloned.1.call-start = ((), (), s32[]{:S(2)}) async-start(), calls=%async_computation.16 | async-start | bytes 3932160 | tf_op jit(solution)/shard_map/all_gather | solution.py:138
  524.1 357.1 %all-gather.37.cloned.1.call-start = ((), (), s32[]{:S(2)}) async-start(), calls=%async_computation.17 | async-start | bytes 3932160 | tf_op jit(solution)/shard_map/all_gather | solution.py:139
  763.0 303.9 %all-gather.39.cloned.1.call-start = ((), (), s32[]{:S(2)}) async-start(), calls=%async_computation.18 | async-start | bytes 3932160 | tf_op jit(solution)/shard_map/all_gather | solution.py:138
  763.8 340.1 %all-gather.41.cloned.1.call-start = ((), (), s32[]{:S(2)}) async-start(), calls=%async_computation.19 | async-start | bytes 3932160 | tf_op jit(solution)/shard_map/all_gather | solution.py:139
  1000.2 293.2 %reduce-scatter.7.cloned.1.call-start = ((), (), s32[]{:S(2)}) async-start(), calls=%async_computation.20 | async-start | bytes 2433024 | tf_op jit(solution)/shard_map/reduce_scatter | solution.py:409
  1066.8 226.6 %reduce-scatter.13.cloned.1.call-start = ((), (), s32[]{:S(2)}) async-start(), calls=%async_computation.23 | async-start | bytes 2433024 | tf_op jit(solution)/shard_map/reduce_scatter | solution.py:409
  1103.9 276.4 %reduce-scatter.9.cloned.1.call-start = ((), (), s32[]{:S(2)}) async-start(), calls=%async_computation.21 | async-start | bytes 2433024 | tf_op jit(solution)/shard_map/reduce_scatter | solution.py:409
  1191.0 293.6 %reduce-scatter.11.cloned.1.call-start = ((), (), s32[]{:S(2)}) async-start(), calls=%async_computation.22 | async-start | bytes 2433024 | tf_op jit(solution)/shard_map/reduce_scatter | solution.py:409
  1203.5 422.6 %reduce-scatter.15.cloned.1.call-start = ((), (), s32[]{:S(2)}) async-start(), calls=%async_computation.24 | async-start | bytes 9732096 | tf_op jit(solution)/shard_map/reduce_scatter | solution.py:409
  1215.9 551.7 %reduce-scatter.17.cloned.1.call-start = ((), (), s32[]{:S(2)}) async-start(), calls=%async_computation.25 | async-start | bytes 9732096 | tf_op jit(solution)/shard_map/reduce_scatter | solution.py:409
  (150 other events, 1641.8 us)
Sparse Core Ops, SparseCore 0:
  10.8 56.4 all-gather.14
  70.1 53.1 all-gather.20
  126.1 53.0 all-gather.18
  181.2 60.4 all-gather.16
  243.0 61.5 all-gather.22
  307.3 54.1 all-gather.24
  364.3 62.4 all-gather.26
  429.6 61.8 all-gather.28
  507.9 59.7 all-gather.30
  569.1 61.5 all-gather.32
  632.3 61.5 all-gather.34
  763.1 63.7 all-gather.36
  828.4 66.1 all-gather.38
  1000.3 67.4 all-gather.40
  1073.6 97.7 reduce-scatter.6
  1177.1 98.7 reduce-scatter.12
  1281.6 98.6 reduce-scatter.8
  1385.9 98.6 reduce-scatter.10
  1491.1 135.0 reduce-scatter.14
  1632.4 135.0 reduce-scatter.16
where the time goes:
time: 1790 us; the launch traced here: 1780 us
  waiting for transfers between devices  910 us (51%)
  matrix products  422 us (24%)
  local copies, waits for them, and re-layouts  172 us (10%)
  blocking collectives  149 us (8%)
  other arithmetic  83.7 us (5%)
  between operations  19 us (1%)
    reduce_scatter x6, waiting for transfers between devices, local(): lax.psum_scatter(total, ('dp', 'ctx'), scatter_dimension=0, tiled=True)  474 us
    all_gather x2, waiting for transfers between devices, attend(): lax.all_gather(valued, 'ctx', axis=0, tiled=True)  118 us
    all_gather x2, waiting for transfers between devices, attend(): lax.all_gather(keyed, 'ctx', axis=0, tiled=True)  99.1 us
    all_gather x1, waiting for transfers between devices, local(): lax.all_gather(shards[11], ('dp', 'ctx'), axis=0, tiled=True)  57.7 us
    all_gather x1, waiting for transfers between devices, local(): lax.all_gather(shards[2], ('dp', 'ctx'), axis=0, tiled=True)  55.5 us
    dot_general x8, matrix products, query_step(): jnp.einsum('cshk,kshd->cshd', d_scores, key_block, preferred_element_type...  54.9 us
    all_gather x1, waiting for transfers between devices, local(): lax.all_gather(shards[9], ('dp', 'ctx'), axis=0, tiled=True)  49.3 us
    dot_general x8, matrix products, key_step(): jnp.einsum('qshk,qshd->kshd', d_scores, query_block, preferred_element_ty...  49.1 us
  transfers between devices with their start and end apart: 20, of which 13 were waited for; matrix products, arithmetic and copies ran while one was open for 37% of the time, Pallas kernels for 0%

commit v1 on v0

v1 whole, which is shorter than its diff:
```python
import functools

import jax
import jax.numpy as jnp
from jax import lax
from jax.experimental import pallas as pl
from jax.experimental.pallas import tpu as pltpu
from jax.sharding import PartitionSpec as P

H = 12
HD = 64
EPSILON = 1e-12
MASKED = -1e30
LOG2E = 1.4426950408889634
AXES = ("dp", "ctx")
BF = jnp.bfloat16
F32 = jnp.float32


def mm(left, right):
    return jnp.dot(left, right, preferred_element_type=F32)


def mm_rows(left, right):
    return lax.dot_general(left, right, (((0,), (0,)), ((), ())), preferred_element_type=F32)


def mm_back(left, right):
    return lax.dot_general(left, right, (((1,), (1,)), ((), ())), preferred_element_type=F32)


def normalize(values, gain, shift):
    centre = values - jnp.mean(values, axis=-1, keepdims=True)
    spread = jnp.mean(centre * centre, axis=-1, keepdims=True)
    return centre * lax.rsqrt(spread + EPSILON) * gain + shift


def activate(values):
    return jax.nn.gelu(values, approximate=True)


def column_sum(values):
    return jnp.sum(values.astype(F32), axis=0)


class Grid:
    def __init__(self, n_dp, n_ctx):
        self.n_dp, self.n_ctx, self.n = n_dp, n_ctx, n_dp * n_ctx
        self.dp, self.ctx = lax.axis_index("dp"), lax.axis_index("ctx")
        self.lin = self.dp * n_ctx + self.ctx
        self.ctx_bits = [1 << i for i in range(n_ctx.bit_length() - 1)]
        self.core_bit = n_ctx
        self.top_bits = [2 * n_ctx << i for i in range(n_dp.bit_length() - 2)]
        self.core = self.dp % 2

    def flip(self, value, mask):
        return lax.ppermute(value, AXES, [(i, i ^ mask) for i in range(self.n)])

    def bit(self, mask):
        return (self.lin // mask) % 2


def gather_ctx(grid, part):
    parts = [part]
    for mask in reversed(grid.ctx_bits):
        sent = jnp.concatenate(parts, 0) if len(parts) > 1 else parts[0]
        got = jnp.split(grid.flip(sent, mask), len(parts), 0)
        low = grid.bit(mask) == 0
        parts = [
            jnp.where(low == first, mine, other)
            for mine, other in zip(parts, got)
            for first in (True, False)
        ]
    return jnp.concatenate(parts, 0)


def gather_top(grid, part):
    width = part.shape[1]
    if len(grid.top_bits) == 2:
        a, b = grid.top_bits
        cut = width // 256 * 128
        by_a, by_b = grid.flip(part, a), grid.flip(part, b)
        left = grid.flip(by_b[:, :cut], a)
        right = grid.flip(by_a[:, cut:], b)
        pieces = [(0, 0, part), (a, 0, by_a), (b, 0, by_b), (a ^ b, 0, left), (a ^ b, cut, right)]
    else:
        pieces = [(0, 0, part)]
        for bit in grid.top_bits:
            pieces = pieces + [(m ^ bit, c, grid.flip(v, bit)) for m, c, v in pieces]
    core = grid.core_bit
    pieces = pieces + [(m ^ core, c, grid.flip(v, core)) for m, c, v in pieces]
    return [(m // grid.n_ctx, c, v) for m, c, v in pieces]


def assemble(grid, pieces, rows, targets, shapes):
    copies = []
    for number, (rel, start, value) in enumerate(pieces):
        for first, columns, array, column, height, offset in targets:
            low, high = max(first, start), min(first + columns, start + value.shape[1])
            if low < high:
                copies.append((number, rel, low - start, high - low, array, column + low - first, height, offset))

    def kernel(me, *refs):
        sources, outs, sems = refs[: len(pieces)], refs[len(pieces) : -1], refs[-1]
        started = []
        for i, (number, rel, source, columns, array, column, height, offset) in enumerate(copies):
            row = pl.multiple_of((me[0] ^ rel) * height + offset, 16)
            copy = pltpu.make_async_copy(
                sources[number].at[:, pl.ds(source, columns)],
                outs[array].at[pl.ds(row, rows), pl.ds(column, columns)],
                sems.at[i],
            )
            copy.start()
            started.append(copy)
        for copy in started:
            copy.wait()

    return pl.pallas_call(
        kernel,
        out_shape=[jax.ShapeDtypeStruct(s, BF) for s in shapes],
        grid_spec=pltpu.PrefetchScalarGridSpec(
            num_scalar_prefetch=1,
            grid=(1,),
            in_specs=[pl.BlockSpec(memory_space=pl.ANY)] * len(pieces),
            out_specs=[pl.BlockSpec(memory_space=pltpu.VMEM)] * len(shapes),
            scratch_shapes=[pltpu.SemaphoreType.DMA((len(copies),))],
        ),
        name="assemble",
    )(grid.dp.reshape(1), *[v for _, _, v in pieces])


def scatter_sum(grid, total):
    rows, width = total.shape
    block = rows // grid.n_dp
    top = grid.n_dp // 2
    pick = functools.partial(lax.dynamic_index_in_dim, keepdims=False)
    value = total.reshape(top, 2, block, width)
    got = grid.flip(pick(value, 1 - grid.core, 1).astype(BF), grid.core_bit)
    value = pick(value, grid.core, 1) + got.astype(F32)

    def step(value, mask, axis):
        bit = grid.bit(mask)
        got = grid.flip(pick(value, 1 - bit, axis).astype(BF), mask)
        return pick(value, bit, axis) + got.astype(F32)

    if len(grid.top_bits) == 2:
        a, b = grid.top_bits
        cut = width // 256 * 128
        value = value.reshape(2, 2, block, width)
        left, right = value[..., :cut], value[..., cut:]
        left = step(step(left, a, 1), b, 0)
        right = step(step(right, b, 0), a, 0)
        value = jnp.concatenate([left, right], -1)
    else:
        for mask in reversed(grid.top_bits):
            value = step(value.reshape(2, value.shape[0] // 2, block, width), mask, 0)
        value = value[0]
    own = block // grid.n_ctx
    for mask in grid.ctx_bits:
        value = step(value.reshape(-1, 2, own, width), mask, 1)
        value = value.reshape(-1, width)
    return value


def lanes(shape):
    return lax.broadcasted_iota(jnp.int32, shape, len(shape) - 1)


def attend_kernel(count, scale, q_ref, mask_ref, *refs):
    k_refs, v_refs = refs[:count], refs[count : 2 * count]
    o_ref, lse_ref = refs[2 * count :]
    rows = q_ref.shape[0]
    factor = scale * LOG2E
    lane = lanes((rows, 128))
    first = lane < HD
    one = jnp.where(lane % HD == 0, 1.0, 0.0).astype(BF)
    outs = []
    for head in range(2):
        keep = first if head == 0 else jnp.logical_not(first)
        query = jnp.where(keep, q_ref[...], one)
        scores = [
            mm_back(jnp.where(keep, k_refs[i][...], mask_ref[i]), query) for i in range(count)
        ]
        top = functools.reduce(jnp.maximum, [jnp.max(s, axis=0, keepdims=True) for s in scores])
        top = top * factor
        mixed = None
        for i in range(count):
            probs = jnp.exp2(scores[i] * factor - top).astype(BF)
            value = jnp.where(keep, v_refs[i][...], jnp.ones((), BF))
            part = mm_rows(value, probs)
            mixed = part if mixed is None else mixed + part
        if head == 0:
            total, mixed = mixed[HD : HD + 1], mixed[:HD]
        else:
            total, mixed = mixed[:1], mixed[HD:]
        outs.append(mixed / total)
        lse_ref[0, head : head + 1, :] = top + jnp.log2(total)
    o_ref[...] = jnp.concatenate(outs, 0).T.astype(BF)


def attend(query, keyed, mask):
    rows, model = query.shape
    count, pairs = len(keyed), model // 128
    at = lambda base: pl.BlockSpec((rows, 128), lambda j: (0, base + j))
    return pl.pallas_call(
        functools.partial(attend_kernel, count, HD**-0.5),
        grid=(pairs,),
        in_specs=[at(0), pl.BlockSpec((count, rows, 128), lambda j: (0, 0, 0))]
        + [at(0)] * count
        + [at(pairs)] * count,
        out_specs=[at(0), pl.BlockSpec((1, 8, rows), lambda j: (j, 0, 0))],
        out_shape=[
            jax.ShapeDtypeStruct((rows, model), BF),
            jax.ShapeDtypeStruct((pairs, 8, rows), F32),
        ],
        compiler_params=pltpu.CompilerParams(vmem_limit_bytes=56 << 20),
        name="attend",
    )(query, mask, *keyed, *keyed)


def attend_back_kernel(count, scale, q_ref, do_ref, o_ref, lse_ref, mask_ref, *refs):
    k_refs, v_refs = refs[:count], refs[count : 2 * count]
    dq_ref = refs[2 * count]
    dk_refs, dv_refs = refs[2 * count + 1 : 3 * count + 1], refs[3 * count + 1 :]
    rows = q_ref.shape[0]
    factor = scale * LOG2E
    lane = lanes((rows, 128))
    first = lane < HD
    one = jnp.where(lane % HD == 0, 1.0, 0.0).astype(BF)
    two = jnp.where(lane % HD < 2, 1.0, 0.0).astype(BF)
    wide = do_ref[...].astype(F32)
    product = wide * o_ref[...].astype(F32)
    d_query = []
    keeps = (first, jnp.logical_not(first))
    d_key = [[None] * 2 for _ in range(count)]
    d_value = [[None] * 2 for _ in range(count)]
    for head in range(2):
        keep = keeps[head]
        query = jnp.where(keep, q_ref[...], one)
        delta = jnp.sum(jnp.where(keep, product, 0.0), axis=1, keepdims=True)
        high = delta.astype(BF).astype(F32)
        spare = lane % HD
        extra = jnp.where(spare == 0, -high, jnp.where(spare == 1, high - delta, 0.0))
        d_out = jnp.where(keep, wide, extra).astype(BF)
        lse = lse_ref[0, head : head + 1, :]
        grad = None
        for i in range(count):
            key = jnp.where(keep, k_refs[i][...], mask_ref[i])
            scores = mm_back(key, query)
            probs = jnp.exp2(scores * factor - lse)
            d_probs = mm_back(jnp.where(keep, v_refs[i][...], two), d_out)
            d_scores = (probs * d_probs).astype(BF)
            d_value[i][head] = mm(probs.astype(BF), do_ref[...])
            d_key[i][head] = mm(d_scores, query)
            part = mm_rows(k_refs[i][...], d_scores)
            grad = part if grad is None else grad + part
        d_query.append(grad[:HD] if head == 0 else grad[HD:])
    dq_ref[...] = (jnp.concatenate(d_query, 0).T * scale).astype(BF)
    for i in range(count):
        dk_refs[i][...] = (jnp.where(first, *d_key[i]) * scale).astype(BF)
        dv_refs[i][...] = jnp.where(first, *d_value[i]).astype(BF)


def attend_back(query, d_mixed, mixed, lse, keyed, mask):
    rows, model = query.shape
    count, pairs = len(keyed), model // 128
    at = lambda base: pl.BlockSpec((rows, 128), lambda j: (0, base + j))
    out = jax.ShapeDtypeStruct((rows, model), BF)
    outs = pl.pallas_call(
        functools.partial(attend_back_kernel, count, HD**-0.5),
        grid=(pairs,),
        in_specs=[at(0)] * 3
        + [pl.BlockSpec((1, 8, rows), lambda j: (j, 0, 0))]
        + [pl.BlockSpec((count, rows, 128), lambda j: (0, 0, 0))]
        + [at(0)] * count
        + [at(pairs)] * count,
        out_specs=[at(0)] * (1 + 2 * count),
        out_shape=[out] * (1 + 2 * count),
        compiler_params=pltpu.CompilerParams(vmem_limit_bytes=56 << 20),
        name="attend_back",
    )(query, d_mixed, mixed, lse, mask, *keyed, *keyed)
    return outs[0], outs[1 : 1 + count], outs[1 + count :]


def forward_layer(grid, group_bits, hidden, params, mask):
    flat_low = hidden.astype(BF)
    keyed = (mm(flat_low, params["kv"]) + params["kv_bias"]).astype(BF)
    pieces = [keyed]
    for bit in group_bits:
        pieces = pieces + [grid.flip(v, bit) for v in pieces]
    query = (mm(flat_low, params["q"]) + params["q_bias"]).astype(BF)
    mixed, lse = attend(query, pieces, mask)
    joined = hidden + mm(mixed, params["out"]) + params["out_bias"]
    first = normalize(joined, params["first_gain"], params["first_shift"])
    first_low = first.astype(BF)
    inner = mm(first_low, params["up"]) + params["up_bias"]
    act_low = activate(inner).astype(BF)
    summed = first + mm(act_low, params["down"]) + params["down_bias"]
    result = normalize(summed, params["second_gain"], params["second_shift"])
    return result, (flat_low, query, pieces, mixed, lse, joined, first_low, inner, act_low, summed)


def backward_layer(grid, group_bits, grad_out, saved, params, mask):
    flat_low, query, pieces, mixed, lse, joined, first_low, inner, act_low, summed = saved
    _, second_back = jax.vjp(normalize, summed, params["second_gain"], params["second_shift"])
    d_summed, d_second_gain, d_second_shift = second_back(grad_out)
    d_down = d_summed.astype(BF)
    d_act = mm_back(d_down, params["down"])
    _, act_back = jax.vjp(activate, inner)
    d_inner = act_back(d_act)[0].astype(BF)
    d_first = d_summed + mm_back(d_inner, params["up"])
    _, first_back = jax.vjp(normalize, joined, params["first_gain"], params["first_shift"])
    d_joined, d_first_gain, d_first_shift = first_back(d_first)
    d_branch = d_joined.astype(BF)
    d_mixed = mm_back(d_branch, params["out"]).astype(BF)
    d_query, d_keys, d_values = attend_back(query, d_mixed, mixed, lse, pieces, mask)
    for bit in reversed(group_bits):
        half = len(d_keys) // 2

        def join(values):
            return [
                (mine.astype(F32) + grid.flip(sent, bit).astype(F32)).astype(BF)
                for mine, sent in zip(values[:half], values[half:])
            ]

        d_keys, d_values = join(d_keys), join(d_values)
    d_key, d_value = d_keys[0], d_values[0]
    model = d_key.shape[1]
    d_hidden = (
        d_joined
        + mm_back(d_query, params["q"])
        + mm_back(d_key, params["kv"][:, :model])
        + mm_back(d_value, params["kv"][:, model:])
    )
    weights = {
        "down": mm_rows(act_low, d_down),
        "out_up": jnp.concatenate([mm_rows(mixed, d_branch), mm_rows(first_low, d_inner)], 1),
        "qkv": mm_rows(flat_low, jnp.concatenate([d_query, d_key, d_value], 1)),
    }
    vectors = (
        column_sum(d_query),
        column_sum(d_value),
        column_sum(d_branch),
        d_first_gain,
        d_first_shift,
        column_sum(d_down),
        d_second_gain,
        d_second_shift,
        column_sum(d_inner),
    )
    return weights, vectors, d_hidden


def local(n_dp, n_ctx, tokens, lengths, teacher, *shards):
    (
        query_weight,
        query_bias,
        key_weight,
        value_weight,
        value_bias,
        out_weight,
        out_bias,
        first_gain,
        first_shift,
        up_weight,
        up_bias,
        down_weight,
        down_bias,
        second_gain,
        second_shift,
    ) = shards
    grid = Grid(n_dp, n_ctx)
    width, seqs, model = tokens.shape
    hidden_units = up_weight.shape[1]
    rows = query_weight.shape[0]
    block = rows * n_ctx

    spread = n_ctx // (2 * seqs)
    mine = grid.ctx // spread
    member = grid.core * spread + grid.ctx % spread
    group_bits = [1 << i for i in range(spread.bit_length() - 1)] + [grid.core_bit]

    def route(turn):
        pairs = []
        for pair in range(n_dp // 2):
            for core in range(2):
                for at in range(n_ctx):
                    seq = core * seqs + (at + turn) % seqs
                    to = at // seqs
                    there = (pair * 2 + to // spread) * n_ctx + seq * spread + to % spread
                    pairs.append(((pair * 2 + core) * n_ctx + at, there))
        return pairs

    def to_groups(values):
        return jnp.concatenate(
            [
                lax.ppermute(
                    lax.dynamic_index_in_dim(values, (grid.ctx + turn) % seqs, 1, keepdims=False),
                    AXES,
                    route(turn),
                )
                for turn in range(seqs)
            ],
            0,
        )

    def from_groups(values):
        got = [
            lax.ppermute(
                values[turn * width : (turn + 1) * width],
                AXES,
                [(there, here) for here, there in route(turn)],
            )
            for turn in range(seqs)
        ]
        return jnp.stack(
            [
                functools.reduce(
                    lambda a, t: jnp.where((grid.ctx + t) % seqs == seq, got[t], a),
                    range(1, seqs),
                    got[0],
                )
                for seq in range(seqs)
            ],
            1,
        )

    vectors = (
        query_bias,
        value_bias,
        out_bias,
        first_gain,
        first_shift,
        down_bias,
        second_gain,
        second_shift,
    )
    small = jnp.concatenate(
        [jnp.stack(vectors, 1), up_bias.reshape(rows, -1), jnp.zeros((rows, 116), BF)], 1
    )
    first_part = jnp.concatenate([query_weight, key_weight, value_weight, small], 1)
    first_part = gather_ctx(grid, first_part)
    start = to_groups(tokens)
    whole_q, whole_kv, whole_small = assemble(
        grid,
        gather_top(grid, first_part),
        block,
        [
            (0, model, 0, 0, block, 0),
            (model, 2 * model, 1, 0, block, 0),
            (3 * model, 128, 2, 0, block, 0),
        ],
        [(model, model), (model, 2 * model), (model, 128)],
    )
    second_part = gather_ctx(grid, jnp.concatenate([out_weight, up_weight], 1))
    third_part = gather_ctx(grid, down_weight)
    folds = third_part.shape[0] // block
    second_part = jnp.concatenate([second_part] + jnp.split(third_part, folds, 0), 1)
    base = model + hidden_units
    whole_out, whole_up, whole_down = assemble(
        grid,
        gather_top(grid, second_part),
        block,
        [(0, model, 0, 0, block, 0), (model, hidden_units, 1, 0, block, 0)]
        + [(base + f * model, model, 2, 0, folds * block, f * block) for f in range(folds)],
        [(model, model), (model, hidden_units), (hidden_units, model)],
    )
    flat_small = whole_small[:, :12].astype(F32)
    by_vector = flat_small[:, :8].T
    params = {
        "q": whole_q,
        "kv": whole_kv,
        "out": whole_out,
        "up": whole_up,
        "down": whole_down,
        "q_bias": by_vector[0],
        "kv_bias": jnp.concatenate([jnp.zeros((model,), F32), by_vector[1]]),
        "out_bias": by_vector[2],
        "first_gain": by_vector[3],
        "first_shift": by_vector[4],
        "down_bias": by_vector[5],
        "second_gain": by_vector[6],
        "second_shift": by_vector[7],
        "up_bias": flat_small[:, 8:12].reshape(hidden_units),
    }

    both = lax.all_gather(lengths, "dp", axis=0, tiled=True)
    length = both[(grid.dp // 2) * 2 * seqs + mine]

    def slots_of(who):
        place = jnp.arange(width, dtype=jnp.int32)
        return jnp.concatenate(
            [width * (seqs * who + (mine + turn) % seqs) + place for turn in range(seqs)]
        )

    live = (slots_of(member) < length).astype(F32)[:, None]
    relative = [0]
    for bit in group_bits:
        relative = relative + [r ^ (spread if bit == grid.core_bit else bit) for r in relative]
    excluded = jnp.stack([jnp.where(slots_of(member ^ r) < length, 0.0, MASKED) for r in relative])
    mask = jnp.where(jnp.arange(128) % HD == 0, excluded[:, :, None], 0.0).astype(BF)

    middle, first_saved = forward_layer(grid, group_bits, start.astype(F32), params, mask)
    result, second_saved = forward_layer(grid, group_bits, middle, params, mask)
    layer_out = from_groups(result.astype(BF))
    diff = (result - to_groups(teacher).astype(F32)) * live
    sums = jnp.zeros((8, 128), F32).at[0, 0].set(jnp.sum(diff * diff)).at[0, 1].set(jnp.sum(live))
    for index in range(grid.n.bit_length() - 1):
        sums = sums + grid.flip(sums, 1 << index)
    loss = sums[0, 0] / (sums[0, 1] * model)

    weights_b, vectors_b, d_middle = backward_layer(
        grid, group_bits, diff, second_saved, params, mask
    )
    weights_a, vectors_a, d_start = backward_layer(
        grid, group_bits, d_middle, first_saved, params, mask
    )
    weights = jax.tree.map(jnp.add, weights_b, weights_a)
    vectors = jax.tree.map(jnp.add, vectors_b, vectors_a)
    small = jnp.concatenate(
        [jnp.stack(vectors[:8], 1), vectors[8].reshape(model, -1), jnp.zeros((model, 116), F32)], 1
    )
    grad_down = scatter_sum(grid, weights["down"])
    grad_out_up = scatter_sum(grid, weights["out_up"])
    grad_rest = scatter_sum(grid, jnp.concatenate([weights["qkv"], small], 1))
    grad_tokens = from_groups(d_start.astype(BF))
    grad_small = grad_rest[:, 3 * model :]
    vector = [grad_small[:, i] for i in range(8)]
    return (
        layer_out,
        loss,
        grad_tokens,
        grad_rest[:, :model],
        vector[0],
        grad_rest[:, model : 2 * model],
        grad_rest[:, 2 * model : 3 * model],
        vector[1],
        grad_out_up[:, :model],
        vector[2],
        vector[3],
        vector[4],
        grad_out_up[:, model:],
        grad_small[:, 8:12].reshape(-1),
        grad_down,
        vector[5],
        vector[6],
        vector[7],
    )


def solution(mesh):
    matrix, vector = P(AXES, None), P(AXES)
    states = P("ctx", "dp", None)
    params = (
        matrix,
        vector,
        matrix,
        matrix,
        vector,
        matrix,
        vector,
        vector,
        vector,
        matrix,
        vector,
        matrix,
        vector,
        vector,
        vector,
    )
    return jax.shard_map(
        functools.partial(local, mesh.shape["dp"], mesh.shape["ctx"]),
        mesh=mesh,
        in_specs=(states, P("dp"), states) + params,
        out_specs=(states, P(), states) + params,
        check_vma=False,
    )
```

time: 1790 us -> 554 us (0.31)
  waiting for transfers between devices: 910 us -> 123 us
  matrix products: 422 us -> 103 us
  blocking collectives: 149 us -> 4.97 us
  local copies, waits for them, and re-layouts: 172 us -> 90.1 us
  Pallas kernels: 0 us -> 79.6 us
  starting transfers between devices: 1.51 us -> 80.3 us
  other arithmetic: 83.7 us -> 57.5 us
    reduce_scatter x6 -> x0, waiting for transfers between devices: 474 us -> none  [local(): lax.psum_scatter(total, ('dp', 'ctx'), scatter_dimension=0, tiled=True)]
    all_gather x14 -> x0, waiting for transfers between devices: 431 us -> none  [the longest x2 118 us: attend(): lax.all_gather(valued, 'ctx', axis=0, tiled=True)]
    dot_general x92 -> x30, matrix products: 422 us -> 103 us  [the longest x8 43 us: mm_rows(): lax.dot_general(left, right, (((0,), (0,)), ((), ())), preferred_element_...]
    ppermute x0 -> x64, waiting for transfers between devices: none -> 123 us  [the longest x56 110 us: flip(): return lax.ppermute(value, AXES, [(i, i ^ mask) for i in range(self.n)])]
    ppermute x0 -> x64, starting transfers between devices: none -> 80.3 us  [the longest x56 61.6 us: flip(): return lax.ppermute(value, AXES, [(i, i ^ mask) for i in range(self.n)])]
    pallas_call x0 -> x6, Pallas kernels: none -> 79.6 us  [the longest x2 38.4 us: attend_back(): pl.pallas_call(functools.partial(attend_back_kernel, count, HD ** (-0.5))...]
    reshape x23 -> x2, local copies, waits for them, and re-layouts: 69.1 us -> 1.36 us  [the longest x1 0.75 us: local(): up_bias.reshape(rows, -1)]
    all_gather x4 -> x0, blocking collectives: 63.9 us -> none  [the longest x2 39.3 us: key_grads(): lax.all_gather(lse, 'ctx', axis=0, tiled=True)]
  transfers between devices with their start and end apart: 20 -> 64, of which waited for: 13 -> 20; matrix products, arithmetic and copies ran while one was open for 37% -> 34% of each run, Pallas kernels for 0% -> 13%
where the time goes in v1:
time: 554 us; the launch traced here: 545 us
  waiting for transfers between devices  123 us (22%)
  matrix products  103 us (19%)
  local copies, waits for them, and re-layouts  90.1 us (16%)
  starting transfers between devices  80.3 us (14%)
  Pallas kernels  79.6 us (14%)
  other arithmetic  57.5 us (10%)
  between operations  6.21 us (1%)
    ppermute x56, waiting for transfers between devices, flip(): return lax.ppermute(value, AXES, [(i, i ^ mask) for i in range(self.n)])  110 us
    ppermute x56, starting transfers between devices, flip(): return lax.ppermute(value, AXES, [(i, i ^ mask) for i in range(self.n)])  61.6 us
    dot_general x8, matrix products, mm_rows(): lax.dot_general(left, right, (((0,), (0,)), ((), ())), preferred_element_...  43 us
    pallas_call x2, Pallas kernels, attend_back(): pl.pallas_call(functools.partial(attend_back_kernel, count, HD ** (-0.5))...  38.4 us
    dot_general x12, matrix products, mm_back(): lax.dot_general(left, right, (((1,), (1,)), ((), ())), preferred_element_...  32.7 us
    pallas_call x2, Pallas kernels, attend(): pl.pallas_call(functools.partial(attend_kernel, count, HD ** (-0.5)), gri...  28.4 us
    dot_general x10, matrix products, mm(): return jnp.dot(left, right, preferred_element_type=F32)  27.7 us
    unnamed x229, local copies, waits for them, and re-layouts  24.6 us
  transfers between devices with their start and end apart: 64, of which 20 were waited for; matrix products, arithmetic and copies ran while one was open for 34% of the time, Pallas kernels for 13%

profile of v1, /device:TPU:1, one launch (start us, length us, event | category | flops | bytes accessed | tf_op | source)
XLA Modules:
  0.0 545.2 jit_solution(4042939557422166537)
XLA Ops:
  15.7 5.5 %constant_dynamic-slice_fusion.1 = (bf16[256,1,768]{2,1,0:T(2,128)(2,1)}, bf16[256,1,768]{2,1,0:T(2,128)(2,1)}, bf16[256,1,768]{2,1,0:T(2,128)(2,1)S(1)}, bf16[256,1,768]{2,1,0:T(2,128)(2,1)S(1)}) fusion(bf16[256,2,768]{2,1,0:T(2,128)(2,1)S(1)} %copy-done.20, s32[]{:T(128)S(6)} %select_n.383, s32[]{:T(128)S(6)} %select_n.384, bf16[256,2,768]{2,1,0:T(2,128)(2,1)} %param.22), kind=kLoop, calls=%fused_computation.222 | loop fusion | bytes 3145736 | tf_op jit(solution)/shard_map/jit(dynamic_index_in_dim)/dynamic_slice | solution.py:398
  27.2 6.8 %collective-permute-done.16 = bf16[96,768]{1,0:T(8,128)(2,1)} collective-permute-done((bf16[96,768]{1,0:T(8,128)(2,1)}, bf16[96,768]{1,0:T(8,128)(2,1)}, u32[]{:S(2)}, u32[]{:S(2)}) %collective-permute-start.16) | collective-permute-done | bytes 147488 | tf_op jit(solution)/shard_map/ppermute | solution.py:57
  48.9 8.0 %collective-permute-start.8 = (bf16[96,2432]{1,0:T(8,128)(2,1)S(1)}, bf16[96,2432]{1,0:T(8,128)(2,1)S(1)}, u32[]{:S(2)}, u32[]{:S(2)}) collective-permute-start(bf16[96,2432]{1,0:T(8,128)(2,1)S(1)} %pad_maximum_fusion.5.refs_0_), channel_id=1, source_target_pairs={{0,4},{1,5},{2,6},{3,7},{4,0},{5,1},{6,2},{7,3},{8,12},{9,13},{10,... | collective-permute-start | bytes 1400840 | tf_op jit(solution)/shard_map/ppermute | solution.py:57
  88.3 18.7 %collective-permute-done.19.refs_2_ = bf16[96,6912]{1,0:T(8,128)(2,1)} collective-permute-done((bf16[96,6912]{1,0:T(8,128)(2,1)}, bf16[96,6912]{1,0:T(8,128)(2,1)}, u32[]{:S(2)}, u32[]{:S(2)}) %collective-permute-start.19) | collective-permute-done | bytes 1327136 | tf_op jit(solution)/shard_map/ppermute | solution.py:57
  112.6 11.0 %collective-permute-done.20.refs_3_ = bf16[96,3456]{1,0:T(8,128)(2,1)S(1)} collective-permute-done((bf16[96,3456]{1,0:T(8,128)(2,1)S(1)}, bf16[96,3456]{1,0:T(8,128)(2,1)S(1)}, u32[]{:S(2)}, u32[]{:S(2)}) %collective-permute-start.20) | collective-permute-done | bytes 663584 | tf_op jit(solution)/shard_map/ppermute | solution.py:57
  145.0 14.1 %attend.2 = (bf16[512,768]{1,0:T(8,128)(2,1)}, f32[6,8,512]{2,1,0:T(8,128)}) custom-call(bf16[512,768]{1,0:T(8,128)(2,1)} %add_convert_fusion.6.q_ref, bf16[2,512,128]{2,1,0:T(8,128)(2,1)} %select_convert_fusion.mask_ref, bf16[512,1536]{1,0:T(8,128)(2,1)} %copy-done.1, bf16[512,1536]{1,0:T(8,128)(2,1)} %copy-done.2, bf16[512,1536]{1,0:T(8,128)(2,1)} %copy-done.1, ...), custom_call_target="tpu_custom_call" | custom-call | tf_op jit(solution)/shard_map/attend/pallas_call | solution.py:205
  159.2 8.6 %assemble.3 = (bf16[768,768]{1,0:T(8,128)(2,1)}, bf16[768,3072]{1,0:T(8,128)(2,1)}, bf16[3072,768]{1,0:T(8,128)(2,1)}) custom-call(s32[1]{0:T(128)} %bitcast.2.me, bf16[96,6912]{1,0:T(8,128)(2,1)} %select_dynamic-update-slice_fusion.refs_0_, bf16[96,6912]{1,0:T(8,128)(2,1)} %collective-permute-done.18.refs_1_, ...), custom_call_target="tpu_custom_call" | custom-call | tf_op jit(solution)/shard_map/assemble/pallas_call | solution.py:118
  195.4 14.2 %attend.3 = (bf16[512,768]{1,0:T(8,128)(2,1)}, f32[6,8,512]{2,1,0:T(8,128)}) custom-call(bf16[512,768]{1,0:T(8,128)(2,1)} %add_convert_fusion.5.q_ref, bf16[2,512,128]{2,1,0:T(8,128)(2,1)} %select_convert_fusion.mask_ref, bf16[512,1536]{1,0:T(8,128)(2,1)} %copy-done.3, bf16[512,1536]{1,0:T(8,128)(2,1)} %collective-permute-done.27.refs_1_.refs_3_, ...), custom_call_target="tpu_custom_call" | custom-call | tf_op jit(solution)/shard_map/attend/pallas_call | solution.py:205
  225.5 7.4 %convert_reduce_fusion.1 = (f32[3072]{0:T(1024)}, bf16[512,3072]{1,0:T(8,128)(2,1)S(1)}) fusion(f32[512,3072]{1,0:T(8,128)S(1)} %fusion.68, f32[3072]{0:T(1024)S(1)} %copy-done.62, bf16[512,768]{1,0:T(8,128)(2,1)S(1)} %get-tuple-element.154, bf16[3072,768]{1,0:T(8,128)(2,1)S(1)} %bitcast.226), kind=kOutput, calls=%fused_computation.20 | convolution fusion | flops 2452091904 | bytes 14966784 | tf_op jit(solution)/shard_map/dot_general | solution.py:29
  243.2 6.3 %fusion.74 = f32[3072,768]{1,0:T(8,128)} fusion(bf16[512,768]{1,0:T(8,128)(2,1)S(1)} %get-tuple-element.154, f32[512,3072]{1,0:T(8,128)S(1)} %fusion.68, f32[3072]{0:T(1024)S(1)} %copy-done.62), kind=kOutput, calls=%fused_computation.264 | convolution fusion | flops 2431647744 | bytes 16527360 | tf_op jit(solution)/shard_map/dot_general | solution.py:25
  260.1 19.4 %attend_back.2 = (bf16[512,768]{1,0:T(8,128)(2,1)}, bf16[512,768]{1,0:T(8,128)(2,1)}, bf16[512,768]{1,0:T(8,128)(2,1)}, bf16[512,768]{1,0:T(8,128)(2,1)}, bf16[512,768]{1,0:T(8,128)(2,1)}) custom-call(bf16[512,768]{1,0:T(8,128)(2,1)} %add_convert_fusion.5.q_ref, bf16[512,768]{1,0:T(8,128)(2,1)} %convolution_convert_fusion.1.do_ref, ...), custom_call_target="tpu_custom_call" | custom-call | tf_op jit(solution)/shard_map/attend_back/pallas_call | solution.py:269
  302.6 7.4 %convert_reduce_fusion = (f32[3072]{0:T(1024)}, bf16[512,3072]{1,0:T(8,128)(2,1)S(1)}) fusion(f32[512,3072]{1,0:T(8,128)S(1)} %bitcast.230, f32[3072]{0:T(1024)S(1)} %copy-done.63, bf16[512,768]{1,0:T(8,128)(2,1)S(1)} %get-tuple-element.152, bf16[3072,768]{1,0:T(8,128)(2,1)S(1)} %bitcast.228), kind=kOutput, calls=%fused_computation.19 | convolution fusion | flops 2452091904 | bytes 14966784 | tf_op jit(solution)/shard_map/dot_general | solution.py:29
  313.7 5.5 %fusion.70 = f32[768,3072]{1,0:T(8,128)} fusion(bf16[512,3072]{1,0:T(8,128)(2,1)S(1)} %get-tuple-element.148, f32[512,768]{1,0:T(8,128)S(1)} %copy-done.6, f32[768]{0:T(1024)S(1)} %copy-done.74, f32[768]{0:T(1024)S(1)} %get-tuple-element.135, f32[512]{0:T(512)S(1)} %copy-done.67, f32[512]{0:T(512)S(1)} %copy-done.48), kind=kOutput, calls=%fused_computation.262 | convolution fusion | flops 2417885184 | bytes 14166016 | tf_op jit(solution)/shard_map/dot_general | solution.py:25
  323.7 19.0 %attend_back.3 = (bf16[512,768]{1,0:T(8,128)(2,1)}, bf16[512,768]{1,0:T(8,128)(2,1)}, bf16[512,768]{1,0:T(8,128)(2,1)}, bf16[512,768]{1,0:T(8,128)(2,1)}, bf16[512,768]{1,0:T(8,128)(2,1)}) custom-call(bf16[512,768]{1,0:T(8,128)(2,1)} %add_convert_fusion.6.q_ref, bf16[512,768]{1,0:T(8,128)(2,1)} %convolution_convert_fusion.do_ref, ...), custom_call_target="tpu_custom_call" | custom-call | tf_op jit(solution)/shard_map/attend_back/pallas_call | solution.py:269
  343.7 7.3 %maximum_add_fusion = f32[4,2,96,3840]{3,2,1,0:T(8,128)S(1)} fusion(f32[4,2,96,3072]{3,2,1,0:T(8,128)} %bitcast.191, f32[4,2,96,768]{3,2,1,0:T(8,128)S(1)} %bitcast.187, f32[4,2,96,3072]{3,2,1,0:T(8,128)} %bitcast.192, f32[4,2,96,768]{3,2,1,0:T(8,128)S(1)} %bitcast.188), kind=kLoop, calls=%fused_computation | loop fusion | flops 8847360 | bytes 35389440 | tf_op jit(solution)/shard_map/add | solution.py:518
  357.7 9.2 %convolution_add_fusion.1 = f32[3072,768]{1,0:T(8,128)S(1)} fusion(f32[3072,768]{1,0:T(8,128)} %fusion.74, bf16[512,768]{1,0:T(8,128)(2,1)S(1)} %copy-done.34, f32[512,3072]{1,0:T(8,128)} %copy-done.88, f32[3072]{0:T(1024)S(1)} %copy-done.63), kind=kOutput, calls=%fused_computation.26 | convolution fusion | flops 2434007040 | bytes 25964544 | tf_op jit(solution)/shard_map/dot_general | solution.py:25
  391.9 6.8 %fusion.18 = f32[768,2304]{1,0:T(8,128)} fusion(bf16[512,768]{1,0:T(8,128)(2,1)} %copy-done.27, bf16[512,768]{1,0:T(8,128)(2,1)} %copy-done.28, bf16[512,768]{1,0:T(8,128)(2,1)} %copy-done.29, bf16[512,768]{1,0:T(8,128)(2,1)} %get-tuple-element.71), kind=kOutput, calls=%fused_computation.41 | convolution fusion | flops 1819017216 | bytes 10223616 | tf_op jit(solution)/shard_map/dot_general | solution.py:25
  404.0 8.1 %convolution_add_fusion = f32[768,2304]{1,0:T(8,128)} fusion(f32[768,2304]{1,0:T(8,128)} %fusion.18, bf16[512,768]{1,0:T(8,128)(2,1)S(1)} %copy-done.24, bf16[512,768]{1,0:T(8,128)(2,1)S(1)} %copy-done.12, bf16[512,768]{1,0:T(8,128)(2,1)S(1)} %add_convert_fusion.2, bf16[512,768]{1,0:T(8,128)(2,1)S(1)} %copy-done.4), kind=kOutput, calls=%fused_computation.25 | convolution fusion | flops 1820786688 | bytes 17301504 | tf_op jit(solution)/shard_map/dot_general | solution.py:25
  412.9 10.4 %concatenate.143 = f32[4,2,96,2432]{3,2,1,0:T(8,128)} concatenate(f32[4,2,96,2304]{3,2,1,0:T(8,128)} %bitcast.182, f32[4,2,96,1]{3,2,1,0:T(8,128)} %add.833, f32[4,2,96,1]{3,2,1,0:T(8,128)} %add.834, f32[4,2,96,1]{3,2,1,0:T(8,128)} %add.835, f32[4,2,96,1]{3,2,1,0:T(8,128)} %add.836, f32[4,2,96,1]{3,2,1,0:T(8,128)} %add.837, f32[4,2,96,1]{3,2,1,0:T(8,128)} %add.838, ...), dimensions={3} | concatenate | bytes 14942208 | tf_op jit(solution)/shard_map/concatenate | solution.py:525
  441.2 8.9 %collective-permute-done.42 = bf16[256,768]{1,0:T(8,128)(2,1)S(1)} collective-permute-done((bf16[256,768]{1,0:T(8,128)(2,1)S(1)}, bf16[256,768]{1,0:T(8,128)(2,1)S(1)}, u32[]{:S(2)}, u32[]{:S(2)}) %collective-permute-start.42) | collective-permute-done | bytes 393248 | tf_op jit(solution)/shard_map/ppermute | solution.py:409
  474.1 7.1 %collective-permute-done.44 = bf16[2,96,1152]{2,1,0:T(8,128)(2,1)} collective-permute-done((bf16[2,96,1152]{2,1,0:T(8,128)(2,1)}, bf16[2,96,1152]{2,1,0:T(8,128)(2,1)}, u32[]{:S(2)}, u32[]{:S(2)}) %collective-permute-start.44) | collective-permute-done | bytes 442400 | tf_op jit(solution)/shard_map/ppermute | solution.py:57
  485.1 13.9 %collective-permute-done.61 = bf16[384,384]{1,0:T(8,128)(2,1)S(1)} collective-permute-done((bf16[384,384]{1,0:T(8,128)(2,1)S(1)}, bf16[384,384]{1,0:T(8,128)(2,1)S(1)}, u32[]{:S(2)}, u32[]{:S(2)}) %collective-permute-start.61) | collective-permute-done | bytes 294944 | tf_op jit(solution)/shard_map/ppermute | solution.py:57
  511.5 7.0 %collective-permute-done.63 = bf16[1,96,768]{2,1,0:T(8,128)(2,1)S(1)} collective-permute-done((bf16[1,96,768]{2,1,0:T(8,128)(2,1)S(1)}, bf16[1,96,768]{2,1,0:T(8,128)(2,1)S(1)}, u32[]{:S(2)}, u32[]{:S(2)}) %collective-permute-start.63) | collective-permute-done | bytes 147488 | tf_op jit(solution)/shard_map/ppermute | solution.py:57
  529.0 6.9 %collective-permute-done.55 = bf16[2,24,3840]{2,1,0:T(8,128)(2,1)S(1)} collective-permute-done((bf16[2,24,3840]{2,1,0:T(8,128)(2,1)S(1)}, bf16[2,24,3840]{2,1,0:T(8,128)(2,1)S(1)}, u32[]{:S(2)}, u32[]{:S(2)}) %collective-permute-start.55) | collective-permute-done | bytes 368672 | tf_op jit(solution)/shard_map/ppermute | solution.py:57
  (556 shorter events, 301.5 us)
Async XLA Ops:
  13.3 27.1 %collective-permute-start.14 = (bf16[24,3840]{1,0:T(8,128)(2,1)S(1)}, bf16[24,3840]{1,0:T(8,128)(2,1)}, u32[]{:S(2)}, u32[]{:S(2)}) collective-permute-start(bf16[24,3840]{1,0:T(8,128)(2,1)S(1)} %constant_dynamic-update-slice_fusion.2), channel_id=1, source_target_pairs={{0,2},{1,3},{2,0},{3,1},{4,6},{5,7},{6,4},{7,5},{8,10},{9,11},{10,... | collective-permute-start | bytes 552968 | tf_op jit(solution)/shard_map/ppermute | solution.py:57
  21.3 26.4 %collective-permute-start = (bf16[256,768]{1,0:T(8,128)(2,1)S(1)}, bf16[256,768]{1,0:T(8,128)(2,1)S(1)}, u32[]{:S(2)}, u32[]{:S(2)}) collective-permute-start(bf16[256,768]{1,0:T(8,128)(2,1)S(1)} %bitcast.204), channel_id=1, source_target_pairs={{0,0},{1,1},{2,4},{3,5},{4,2},{5,3},{6,6},{7,7},{8,8},{9,9},{10,12... | collective-permute-start | bytes 1179656 | tf_op jit(solution)/shard_map/ppermute | solution.py:397
  24.6 24.3 %collective-permute-start.1 = (bf16[256,768]{1,0:T(8,128)(2,1)S(1)}, bf16[256,768]{1,0:T(8,128)(2,1)S(1)}, u32[]{:S(2)}, u32[]{:S(2)}) collective-permute-start(bf16[256,768]{1,0:T(8,128)(2,1)S(1)} %bitcast.203), channel_id=1, source_target_pairs={{0,1},{1,0},{2,5},{3,4},{4,3},{5,2},{6,7},{7,6},{8,9},{9,8},{10,13... | collective-permute-start | bytes 1179656 | tf_op jit(solution)/shard_map/ppermute | solution.py:397
  35.0 27.8 %collective-permute-start.17 = (bf16[192,768]{1,0:T(8,128)(2,1)S(1)}, bf16[192,768]{1,0:T(8,128)(2,1)S(1)}, u32[]{:S(2)}, u32[]{:S(2)}) collective-permute-start(bf16[192,768]{1,0:T(8,128)(2,1)S(1)} %pad_maximum_fusion.7), channel_id=1, source_target_pairs={{0,1},{1,0},{2,3},{3,2},{4,5},{5,4},{6,7},{7,6},{8,9},{9,8},{10,11... | collective-permute-start | bytes 884744 | tf_op jit(solution)/shard_map/ppermute | solution.py:57
  48.9 26.3 %collective-permute-start.8 = (bf16[96,2432]{1,0:T(8,128)(2,1)S(1)}, bf16[96,2432]{1,0:T(8,128)(2,1)S(1)}, u32[]{:S(2)}, u32[]{:S(2)}) collective-permute-start(bf16[96,2432]{1,0:T(8,128)(2,1)S(1)} %pad_maximum_fusion.5.refs_0_), channel_id=1, source_target_pairs={{0,4},{1,5},{2,6},{3,7},{4,0},{5,1},{6,2},{7,3},{8,12},{9,13},{10,... | collective-permute-start | bytes 1400840 | tf_op jit(solution)/shard_map/ppermute | solution.py:57
  75.2 33.4 %collective-permute-start.18 = (bf16[96,6912]{1,0:T(8,128)(2,1)}, bf16[96,6912]{1,0:T(8,128)(2,1)}, u32[]{:S(2)}, u32[]{:S(2)}) collective-permute-start(bf16[96,6912]{1,0:T(8,128)(2,1)} %select_dynamic-update-slice_fusion.refs_0_), channel_id=1, source_target_pairs={{0,8},{1,9},{2,10},{3,11},{4,12},{5,13},{6,14},{7,15},{8,0},{9,1},... | collective-permute-start | bytes 3981320 | tf_op jit(solution)/shard_map/ppermute | solution.py:57
  76.4 30.7 %collective-permute-start.19 = (bf16[96,6912]{1,0:T(8,128)(2,1)}, bf16[96,6912]{1,0:T(8,128)(2,1)}, u32[]{:S(2)}, u32[]{:S(2)}) collective-permute-start(bf16[96,6912]{1,0:T(8,128)(2,1)} %select_dynamic-update-slice_fusion.refs_0_), channel_id=1, source_target_pairs={{0,16},{1,17},{2,18},{3,19},{4,20},{5,21},{6,22},{7,23},{8,24},{9,... | collective-permute-start | bytes 3981320 | tf_op jit(solution)/shard_map/ppermute | solution.py:57
  87.7 50.8 %collective-permute-start.13 = (bf16[512,1536]{1,0:T(8,128)(2,1)S(1)}, bf16[512,1536]{1,0:T(8,128)(2,1)S(1)}, u32[]{:S(2)}, u32[]{:S(2)}) collective-permute-start(bf16[512,1536]{1,0:T(8,128)(2,1)S(1)} %fusion.14.refs_0_.refs_2_), channel_id=1, source_target_pairs={{0,4},{1,5},{2,6},{3,7},{4,0},{5,1},{6,2},{7,3},{8,12},{9,13},{10,... | collective-permute-start | bytes 4718600 | tf_op jit(solution)/shard_map/ppermute | solution.py:57
  110.6 25.8 %collective-permute-start.21 = (bf16[96,3456]{1,0:T(8,128)(2,1)}, bf16[96,3456]{1,0:T(8,128)(2,1)}, u32[]{:S(2)}, u32[]{:S(2)}) collective-permute-start(bf16[96,3456]{1,0:T(8,128)(2,1)} %slice.229), channel_id=1, source_target_pairs={{0,16},{1,17},{2,18},{3,19},{4,20},{5,21},{6,22},{7,23},{8,24},{9,... | collective-permute-start | bytes 1990664 | tf_op jit(solution)/shard_map/ppermute | solution.py:57
  110.9 48.3 %collective-permute-start.22 = (bf16[96,6912]{1,0:T(8,128)(2,1)}, bf16[96,6912]{1,0:T(8,128)(2,1)}, u32[]{:S(2)}, u32[]{:S(2)}) collective-permute-start(bf16[96,6912]{1,0:T(8,128)(2,1)} %select_dynamic-update-slice_fusion.refs_0_), channel_id=1, source_target_pairs={{0,4},{1,5},{2,6},{3,7},{4,0},{5,1},{6,2},{7,3},{8,12},{9,13},{10,... | collective-permute-start | bytes 3981320 | tf_op jit(solution)/shard_map/ppermute | solution.py:57
  112.6 46.5 %collective-permute-start.23 = (bf16[96,6912]{1,0:T(8,128)(2,1)}, bf16[96,6912]{1,0:T(8,128)(2,1)}, u32[]{:S(2)}, u32[]{:S(2)}) collective-permute-start(bf16[96,6912]{1,0:T(8,128)(2,1)} %collective-permute-done.18.refs_1_), channel_id=1, source_target_pairs={{0,4},{1,5},{2,6},{3,7},{4,0},{5,1},{6,2},{7,3},{8,12},{9,13},{10,... | collective-permute-start | bytes 3981320 | tf_op jit(solution)/shard_map/ppermute | solution.py:57
  124.5 34.7 %collective-permute-start.24 = (bf16[96,6912]{1,0:T(8,128)(2,1)}, bf16[96,6912]{1,0:T(8,128)(2,1)}, u32[]{:S(2)}, u32[]{:S(2)}) collective-permute-start(bf16[96,6912]{1,0:T(8,128)(2,1)} %collective-permute-done.19.refs_2_), channel_id=1, source_target_pairs={{0,4},{1,5},{2,6},{3,7},{4,0},{5,1},{6,2},{7,3},{8,12},{9,13},{10,... | collective-permute-start | bytes 3981320 | tf_op jit(solution)/shard_map/ppermute | solution.py:57
  182.6 37.9 %collective-permute-start.31 = (bf16[256,768]{1,0:T(8,128)(2,1)}, bf16[256,768]{1,0:T(8,128)(2,1)S(1)}, u32[]{:S(2)}, u32[]{:S(2)}) collective-permute-start(bf16[256,768]{1,0:T(8,128)(2,1)} %bitcast.176), channel_id=1, source_target_pairs={{0,1},{1,0},{2,5},{3,4},{4,3},{5,2},{6,7},{7,6},{8,9},{9,8},{10,13... | collective-permute-start | bytes 1179656 | tf_op jit(solution)/shard_map/ppermute | solution.py:397
  186.2 34.3 %collective-permute-start.30 = (bf16[256,768]{1,0:T(8,128)(2,1)}, bf16[256,768]{1,0:T(8,128)(2,1)}, u32[]{:S(2)}, u32[]{:S(2)}) collective-permute-start(bf16[256,768]{1,0:T(8,128)(2,1)} %bitcast.177), channel_id=1, source_target_pairs={{0,0},{1,1},{2,4},{3,5},{4,2},{5,3},{6,6},{7,7},{8,8},{9,9},{10,12... | collective-permute-start | bytes 1179656 | tf_op jit(solution)/shard_map/ppermute | solution.py:397
  283.8 146.2 %collective-permute-start.28 = (bf16[256,768]{1,0:T(8,128)(2,1)}, bf16[256,768]{1,0:T(8,128)(2,1)}, u32[]{:S(2)}, u32[]{:S(2)}) collective-permute-start(bf16[256,768]{1,0:T(8,128)(2,1)} %get-tuple-element.186), channel_id=1, source_target_pairs={{1,0},{0,1},{5,2},{4,3},{3,4},{2,5},{7,6},{6,7},{9,8},{8,9},{13,10... | collective-permute-start | bytes 1179656 | tf_op jit(solution)/shard_map/ppermute | solution.py:409
  285.9 145.4 %collective-permute-start.29 = (bf16[256,768]{1,0:T(8,128)(2,1)}, bf16[256,768]{1,0:T(8,128)(2,1)}, u32[]{:S(2)}, u32[]{:S(2)}) collective-permute-start(bf16[256,768]{1,0:T(8,128)(2,1)} %get-tuple-element.185), channel_id=1, source_target_pairs={{0,0},{1,1},{4,2},{5,3},{2,4},{3,5},{6,6},{7,7},{8,8},{9,9},{12,10... | collective-permute-start | bytes 1179656 | tf_op jit(solution)/shard_map/ppermute | solution.py:409
  342.7 56.0 %collective-permute-start.40 = (bf16[512,768]{1,0:T(8,128)(2,1)}, bf16[512,768]{1,0:T(8,128)(2,1)}, u32[]{:S(2)}, u32[]{:S(2)}) collective-permute-start(bf16[512,768]{1,0:T(8,128)(2,1)} %get-tuple-element.81), channel_id=1, source_target_pairs={{0,4},{1,5},{2,6},{3,7},{4,0},{5,1},{6,2},{7,3},{8,12},{9,13},{10,... | collective-permute-start | bytes 2359304 | tf_op jit(solution)/shard_map/ppermute | solution.py:57
  343.6 58.5 %collective-permute-start.39 = (bf16[512,768]{1,0:T(8,128)(2,1)}, bf16[512,768]{1,0:T(8,128)(2,1)}, u32[]{:S(2)}, u32[]{:S(2)}) collective-permute-start(bf16[512,768]{1,0:T(8,128)(2,1)} %get-tuple-element.79), channel_id=1, source_target_pairs={{0,4},{1,5},{2,6},{3,7},{4,0},{5,1},{6,2},{7,3},{8,12},{9,13},{10,... | collective-permute-start | bytes 2359304 | tf_op jit(solution)/shard_map/ppermute | solution.py:57
  357.2 104.0 %collective-permute-start.50 = (bf16[4,96,3840]{2,1,0:T(8,128)(2,1)}, bf16[4,96,3840]{2,1,0:T(8,128)(2,1)}, u32[]{:S(2)}, u32[]{:S(2)}) collective-permute-start(bf16[4,96,3840]{2,1,0:T(8,128)(2,1)} %fusion.16), channel_id=1, source_target_pairs={{0,4},{1,5},{2,6},{3,7},{4,0},{5,1},{6,2},{7,3},{8,12},{9,13},{10,... | collective-permute-start | bytes 8847368 | tf_op jit(solution)/shard_map/ppermute | solution.py:57
  398.7 53.2 %collective-permute-start.57 = (bf16[4,384,768]{2,1,0:T(8,128)(2,1)}, bf16[4,384,768]{2,1,0:T(8,128)(2,1)}, u32[]{:S(2)}, u32[]{:S(2)}) collective-permute-start(bf16[4,384,768]{2,1,0:T(8,128)(2,1)} %fusion.17), channel_id=1, source_target_pairs={{0,4},{1,5},{2,6},{3,7},{4,0},{5,1},{6,2},{7,3},{8,12},{9,13},{10,... | collective-permute-start | bytes 7077896 | tf_op jit(solution)/shard_map/ppermute | solution.py:57
  426.9 30.4 %collective-permute-start.43 = (bf16[4,96,2432]{2,1,0:T(8,128)(2,1)}, bf16[4,96,2432]{2,1,0:T(8,128)(2,1)S(1)}, u32[]{:S(2)}, u32[]{:S(2)}) collective-permute-start(bf16[4,96,2432]{2,1,0:T(8,128)(2,1)} %fusion.29), channel_id=1, source_target_pairs={{0,4},{1,5},{2,6},{3,7},{4,0},{5,1},{6,2},{7,3},{8,12},{9,13},{10,... | collective-permute-start | bytes 5603336 | tf_op jit(solution)/shard_map/ppermute | solution.py:57
  464.2 55.1 %collective-permute-start.53 = (bf16[2,96,1920]{2,1,0:T(8,128)(2,1)S(1)}, bf16[2,96,1920]{2,1,0:T(8,128)(2,1)S(1)}, u32[]{:S(2)}, u32[]{:S(2)}) collective-permute-start(bf16[2,96,1920]{2,1,0:T(8,128)(2,1)S(1)} %fusion.43), channel_id=1, source_target_pairs={{0,16},{1,17},{2,18},{3,19},{4,20},{5,21},{6,22},{7,23},{8,24},{9,... | collective-permute-start | bytes 2211848 | tf_op jit(solution)/shard_map/ppermute | solution.py:57
  470.1 50.3 %collective-permute-start.51 = (bf16[2,96,1920]{2,1,0:T(8,128)(2,1)S(1)}, bf16[2,96,1920]{2,1,0:T(8,128)(2,1)S(1)}, u32[]{:S(2)}, u32[]{:S(2)}) collective-permute-start(bf16[2,96,1920]{2,1,0:T(8,128)(2,1)S(1)} %fusion.42), channel_id=1, source_target_pairs={{0,8},{1,9},{2,10},{3,11},{4,12},{5,13},{6,14},{7,15},{8,0},{9,1},... | collective-permute-start | bytes 2211848 | tf_op jit(solution)/shard_map/ppermute | solution.py:57
  472.3 26.7 %collective-permute-start.61 = (bf16[384,384]{1,0:T(8,128)(2,1)S(1)}, bf16[384,384]{1,0:T(8,128)(2,1)S(1)}, u32[]{:S(2)}, u32[]{:S(2)}) collective-permute-start(bf16[384,384]{1,0:T(8,128)(2,1)S(1)} %fusion.52), channel_id=1, source_target_pairs={{0,8},{1,9},{2,10},{3,11},{4,12},{5,13},{6,14},{7,15},{8,0},{9,1},... | collective-permute-start | bytes 884744 | tf_op jit(solution)/shard_map/ppermute | solution.py:57
  (149 other events, 1330.8 us)

commit v2 on v1

v2 whole, which is shorter than its diff:
```python
import functools

import jax
import jax.numpy as jnp
from jax import lax
from jax.experimental import pallas as pl
from jax.experimental.pallas import tpu as pltpu
from jax.sharding import PartitionSpec as P

H = 12
HD = 64
EPSILON = 1e-12
MASKED = -1e30
LOG2E = 1.4426950408889634
AXES = ("dp", "ctx")
BF = jnp.bfloat16
F32 = jnp.float32


def mm(left, right):
    return jnp.dot(left, right, preferred_element_type=F32)


def mm_rows(left, right):
    return lax.dot_general(left, right, (((0,), (0,)), ((), ())), preferred_element_type=F32)


def mm_back(left, right):
    return lax.dot_general(left, right, (((1,), (1,)), ((), ())), preferred_element_type=F32)


def normalize(values, gain, shift):
    centre = values - jnp.mean(values, axis=-1, keepdims=True)
    spread = jnp.mean(centre * centre, axis=-1, keepdims=True)
    return centre * lax.rsqrt(spread + EPSILON) * gain + shift


def activate(values):
    return jax.nn.gelu(values, approximate=True)


def column_sum(values):
    return jnp.sum(values.astype(F32), axis=0)


class Grid:
    def __init__(self, n_dp, n_ctx):
        self.n_dp, self.n_ctx, self.n = n_dp, n_ctx, n_dp * n_ctx
        self.dp, self.ctx = lax.axis_index("dp"), lax.axis_index("ctx")
        self.lin = self.dp * n_ctx + self.ctx
        self.ctx_bits = [1 << i for i in range(n_ctx.bit_length() - 1)]
        self.core_bit = n_ctx
        self.top_bits = [2 * n_ctx << i for i in range(n_dp.bit_length() - 2)]
        self.core = self.dp % 2

    def flip(self, value, mask):
        return lax.ppermute(value, AXES, [(i, i ^ mask) for i in range(self.n)])

    def bit(self, mask):
        return (self.lin // mask) % 2


def after(value, *others):
    return lax.optimization_barrier((value, others))[0]


def join_ctx(grid, parts, got, mask):
    got = jnp.split(got, len(parts), 0)
    low = grid.bit(mask) == 0
    return [
        jnp.where(low == first, mine, other)
        for mine, other in zip(parts, got)
        for first in (True, False)
    ]


def side_by_side(parts, axis=0):
    return jnp.concatenate(parts, axis) if len(parts) > 1 else parts[0]


class Gather:
    def __init__(self, grid, part):
        self.grid, self.part = grid, part
        self.pair = len(grid.top_bits) == 2
        self.cut = part.shape[1] // 256 * 128

    def cross(self, value):
        return self.grid.flip(value, self.grid.core_bit)

    def first(self):
        if self.pair:
            moved = [self.grid.flip(self.part, bit) for bit in self.grid.top_bits]
            return moved, self.cross(self.part)
        pieces = [(0, self.part)]
        for bit in self.grid.top_bits:
            pieces += [(m ^ bit, self.grid.flip(v, bit)) for m, v in pieces]
        self.masks = [m for m, _ in pieces]
        return [v for _, v in pieces], [self.cross(v) for _, v in pieces]

    def second(self, moved, crossed):
        if not self.pair:
            return moved, crossed
        by_a, by_b = moved
        a, b = self.grid.top_bits
        left = self.grid.flip(by_b[:, : self.cut], a)
        right = self.grid.flip(by_a[:, self.cut :], b)
        return [by_a, by_b, left, right], [crossed, self.cross(jnp.concatenate(moved, 0))]

    def finish(self, moved, crossed):
        core = self.grid.core_bit
        if self.pair:
            a, b = self.grid.top_bits
            own, both = crossed
            masks, starts = [0, a, b, a ^ b, a ^ b], [0, 0, 0, 0, self.cut]
            sides = jnp.split(both, 2, 0)
            crossed = [own, *sides, self.cross(moved[2]), self.cross(moved[3])]
            moved = [self.part, *moved]
        else:
            masks, starts = self.masks, [0] * len(moved)
        pieces = list(zip(masks, starts, moved))
        pieces += [(m ^ core, c, v) for m, c, v in zip(masks, starts, crossed)]
        return [(m // self.grid.n_ctx, c, v) for m, c, v in pieces]


def meet(*values):
    return lax.optimization_barrier(values)


def assemble(grid, pieces, rows, targets, shapes):
    copies = []
    for number, (rel, start, value) in enumerate(pieces):
        for first, columns, array, column, height, offset in targets:
            low, high = max(first, start), min(first + columns, start + value.shape[1])
            if low < high:
                copies.append((number, rel, low - start, high - low, array, column + low - first, height, offset))

    def kernel(me, *refs):
        sources, outs, sems = refs[: len(pieces)], refs[len(pieces) : -1], refs[-1]
        started = []
        for i, (number, rel, source, columns, array, column, height, offset) in enumerate(copies):
            row = pl.multiple_of((me[0] ^ rel) * height + offset, 16)
            copy = pltpu.make_async_copy(
                sources[number].at[:, pl.ds(source, columns)],
                outs[array].at[pl.ds(row, rows), pl.ds(column, columns)],
                sems.at[i],
            )
            copy.start()
            started.append(copy)
        for copy in started:
            copy.wait()

    return pl.pallas_call(
        kernel,
        out_shape=[jax.ShapeDtypeStruct(s, BF) for s in shapes],
        grid_spec=pltpu.PrefetchScalarGridSpec(
            num_scalar_prefetch=1,
            grid=(1,),
            in_specs=[pl.BlockSpec(memory_space=pl.ANY)] * len(pieces),
            out_specs=[pl.BlockSpec(memory_space=pltpu.VMEM)] * len(shapes),
            scratch_shapes=[pltpu.SemaphoreType.DMA((len(copies),))],
        ),
        name="assemble",
    )(grid.dp.reshape(1), *[v for _, _, v in pieces])


def grads_kernel(count, top, whole, core, *refs):
    lefts, rights = refs[:count], refs[count : 2 * count]
    send, keep, total = refs[-3:]
    block = total.shape[0] // (2 * (top if whole else 1))
    total[...] = sum(mm_rows(left[...], right[...]) for left, right in zip(lefts, rights))
    for i in range(top if whole else 1):
        theirs = pl.multiple_of((2 * i + 1 - core[0]) * block, 8)
        ours = pl.multiple_of((2 * i + core[0]) * block, 8)
        send[i] = total[pl.ds(theirs, block), :].astype(BF)
        keep[i] = total[pl.ds(ours, block), :]


def grads(grid, lefts, rights, columns=None, column=0, into=None):
    rows, height = lefts[0].shape
    width = rights[0].shape[1]
    columns = width if columns is None else columns
    count, top = len(lefts), grid.n_dp // 2
    block = height // (2 * top)
    whole = 2 * block % 128 != 0
    if whole:
        tile = width if width < 1536 else 768
        steps, tall, base = width // tile, height, column // tile
        left = pl.BlockSpec((rows, height), lambda i, c: (0, 0))
        right = pl.BlockSpec((rows, tile), lambda i, c: (0, i))
        out = pl.BlockSpec((top, block, tile), lambda i, c: (0, 0, base + i))
    else:
        tile, steps, tall = width, top, 2 * block
        left = pl.BlockSpec((rows, tall), lambda i, c: (0, i))
        right = pl.BlockSpec((rows, width), lambda i, c: (0, 0))
        out = pl.BlockSpec((1, block, width), lambda i, c: (i, 0, 0))
    earlier = [] if into is None else list(into)
    return pl.pallas_call(
        functools.partial(grads_kernel, count, top, whole),
        out_shape=[
            jax.ShapeDtypeStruct((top, block, columns), BF),
            jax.ShapeDtypeStruct((top, block, columns), F32),
        ],
        grid_spec=pltpu.PrefetchScalarGridSpec(
            num_scalar_prefetch=1,
            grid=(steps,),
            in_specs=[left] * count
            + [right] * count
            + [pl.BlockSpec(memory_space=pl.ANY)] * len(earlier),
            out_specs=[out] * 2,
            scratch_shapes=[pltpu.VMEM((tall, tile), F32)],
        ),
        input_output_aliases={1 + 2 * count + i: i for i in range(len(earlier))},
        compiler_params=pltpu.CompilerParams(vmem_limit_bytes=56 << 20),
        name="grads",
    )(grid.core.reshape(1), *lefts, *rights, *earlier)


class Reduce:
    def __init__(self, grid):
        self.grid, self.sends, self.parts = grid, [], []

    def add(self, send, keep):
        self.parts.append((keep, self.grid.flip(send, self.grid.core_bit)))

    def step(self, value, mask, axis):
        bit = self.grid.bit(mask)
        pick = functools.partial(lax.dynamic_index_in_dim, axis=axis, keepdims=False)
        send = pick(value, 1 - bit).astype(BF)
        self.sends = self.sends + [send]
        return pick(value, bit), self.grid.flip(send, mask)

    def sent(self):
        sends, self.sends = self.sends, []
        return sends

    def first(self, *others):
        got = after([g for _, g in self.parts], *others)
        value = side_by_side([k + g.astype(F32) for (k, _), g in zip(self.parts, got)], -1)
        top, self.block, self.width = value.shape
        if len(self.grid.top_bits) == 2:
            a, b = self.grid.top_bits
            cut = self.width // 256 * 128
            value = value.reshape(2, 2, self.block, self.width)
            self.halves = [self.step(value[..., :cut], a, 1), self.step(value[..., cut:], b, 0)]
        else:
            for mask in reversed(self.grid.top_bits):
                value = value.reshape(2, value.shape[0] // 2, self.block, self.width)
                keep, got = self.step(value, mask, 0)
                value = keep + got.astype(F32)
            self.halves = [(value[0], None)]

    def second(self, *others):
        if len(self.halves) == 2:
            a, b = self.grid.top_bits
            (left, by_a), (right, by_b) = self.halves
            by_a, by_b = after((by_a, by_b), *others)
            self.halves = [
                self.step(left + by_a.astype(F32), b, 0),
                self.step(right + by_b.astype(F32), a, 0),
            ]

    def third(self, *others):
        values = [k if g is None else k + after(g, *others).astype(F32) for k, g in self.halves]
        self.value = side_by_side(values, -1)
        self.left = list(self.grid.ctx_bits)
        self.turn()

    def turn(self):
        own = self.block // self.grid.n_ctx
        self.last = self.step(self.value.reshape(-1, 2, own, self.width), self.left.pop(0), 1)

    def fourth(self, *others):
        keep, got = self.last
        self.last = None
        self.value = (keep + after(got, *others).astype(F32)).reshape(-1, self.width)
        if self.left:
            self.turn()

    def finish_value(self):
        while self.last is not None:
            self.fourth()
        return self.value


def lanes(shape):
    return lax.broadcasted_iota(jnp.int32, shape, len(shape) - 1)


def attend_kernel(count, scale, q_ref, mask_ref, *refs):
    k_refs, v_refs = refs[:count], refs[count : 2 * count]
    o_ref, lse_ref = refs[2 * count :]
    rows = q_ref.shape[0]
    factor = scale * LOG2E
    lane = lanes((rows, 128))
    first = lane < HD
    one = jnp.where(lane % HD == 0, 1.0, 0.0).astype(BF)
    outs = []
    for head in range(2):
        keep = first if head == 0 else jnp.logical_not(first)
        query = jnp.where(keep, q_ref[...], one)
        scores = [
            mm_back(jnp.where(keep, k_refs[i][...], mask_ref[i]), query) for i in range(count)
        ]
        top = functools.reduce(jnp.maximum, [jnp.max(s, axis=0, keepdims=True) for s in scores])
        top = top * factor
        mixed = None
        for i in range(count):
            probs = jnp.exp2(scores[i] * factor - top).astype(BF)
            value = jnp.where(keep, v_refs[i][...], jnp.ones((), BF))
            part = mm_rows(value, probs)
            mixed = part if mixed is None else mixed + part
        if head == 0:
            total, mixed = mixed[HD : HD + 1], mixed[:HD]
        else:
            total, mixed = mixed[:1], mixed[HD:]
        outs.append(mixed / total)
        lse_ref[0, head : head + 1, :] = top + jnp.log2(total)
    o_ref[...] = jnp.concatenate(outs, 0).T.astype(BF)


def attend(query, keyed, mask, begin=0, pairs=None, into=None):
    rows, model = query.shape
    count, every = len(keyed), model // 128
    pairs = every if pairs is None else pairs
    at = lambda base: pl.BlockSpec((rows, 128), lambda j: (0, base + begin + j))
    earlier = [] if into is None else list(into)

    def kernel(*refs):
        inputs = 2 + 2 * count
        attend_kernel(count, HD**-0.5, *refs[:inputs], *refs[inputs + len(earlier) :])

    return pl.pallas_call(
        kernel,
        grid=(pairs,),
        in_specs=[at(0), pl.BlockSpec((count, rows, 128), lambda j: (0, 0, 0))]
        + [at(0)] * count
        + [at(every)] * count
        + [pl.BlockSpec(memory_space=pl.ANY)] * len(earlier),
        out_specs=[at(0), pl.BlockSpec((1, 8, rows), lambda j: (begin + j, 0, 0))],
        out_shape=[
            jax.ShapeDtypeStruct((rows, model), BF),
            jax.ShapeDtypeStruct((every, 8, rows), F32),
        ],
        input_output_aliases={2 + 2 * count + i: i for i in range(len(earlier))},
        compiler_params=pltpu.CompilerParams(vmem_limit_bytes=56 << 20),
        name="attend",
    )(query, mask, *keyed, *keyed, *earlier)


def attend_back_kernel(count, scale, q_ref, do_ref, o_ref, lse_ref, mask_ref, *refs):
    k_refs, v_refs = refs[:count], refs[count : 2 * count]
    dq_ref = refs[2 * count]
    dkv_refs = refs[2 * count + 1 :]
    rows = q_ref.shape[0]
    factor = scale * LOG2E
    lane = lanes((rows, 128))
    first = lane < HD
    one = jnp.where(lane % HD == 0, 1.0, 0.0).astype(BF)
    two = jnp.where(lane % HD < 2, 1.0, 0.0).astype(BF)
    wide = do_ref[...].astype(F32)
    product = wide * o_ref[...].astype(F32)
    d_query = []
    keeps = (first, jnp.logical_not(first))
    d_key = [[None] * 2 for _ in range(count)]
    d_value = [[None] * 2 for _ in range(count)]
    for head in range(2):
        keep = keeps[head]
        query = jnp.where(keep, q_ref[...], one)
        delta = jnp.sum(jnp.where(keep, product, 0.0), axis=1, keepdims=True)
        high = delta.astype(BF).astype(F32)
        spare = lane % HD
        extra = jnp.where(spare == 0, -high, jnp.where(spare == 1, high - delta, 0.0))
        d_out = jnp.where(keep, wide, extra).astype(BF)
        lse = lse_ref[0, head : head + 1, :]
        grad = None
        for i in range(count):
            key = jnp.where(keep, k_refs[i][...], mask_ref[i])
            scores = mm_back(key, query)
            probs = jnp.exp2(scores * factor - lse)
            d_probs = mm_back(jnp.where(keep, v_refs[i][...], two), d_out)
            d_scores = (probs * d_probs).astype(BF)
            d_value[i][head] = mm(probs.astype(BF), do_ref[...])
            d_key[i][head] = mm(d_scores, query)
            part = mm_rows(k_refs[i][...], d_scores)
            grad = part if grad is None else grad + part
        d_query.append(grad[:HD] if head == 0 else grad[HD:])
    dq_ref[...] = (jnp.concatenate(d_query, 0).T * scale).astype(BF)
    for i in range(count):
        dkv_refs[i][0] = (jnp.where(first, *d_key[i]) * scale).astype(BF)
        dkv_refs[i][1] = jnp.where(first, *d_value[i]).astype(BF)


def attend_back(query, d_mixed, mixed, lse, keyed, mask, begin, pairs):
    rows, model = query.shape
    count, every = len(keyed), model // 128
    at = lambda base: pl.BlockSpec((rows, 128), lambda j: (0, base + begin + j))
    outs = pl.pallas_call(
        functools.partial(attend_back_kernel, count, HD**-0.5),
        grid=(pairs,),
        in_specs=[at(0)] * 3
        + [pl.BlockSpec((1, 8, rows), lambda j: (begin + j, 0, 0))]
        + [pl.BlockSpec((count, rows, 128), lambda j: (0, 0, 0))]
        + [at(0)] * count
        + [at(every)] * count,
        out_specs=[pl.BlockSpec((rows, 128), lambda j: (0, j))]
        + [pl.BlockSpec((2, rows, 128), lambda j: (0, 0, j))] * count,
        out_shape=[jax.ShapeDtypeStruct((rows, pairs * 128), BF)]
        + [jax.ShapeDtypeStruct((2, rows, pairs * 128), BF)] * count,
        compiler_params=pltpu.CompilerParams(vmem_limit_bytes=56 << 20),
        name="attend_back",
    )(query, d_mixed, mixed, lse, mask, *keyed, *keyed)
    return outs[0], list(outs[1:])


def forward_layer(grid, group_bits, hidden, params, mask, hooks=None):
    flat_low = hidden.astype(BF)
    keyed = (mm(flat_low, params["kv"]) + params["kv_bias"]).astype(BF)
    pieces = [keyed]
    for bit in group_bits:
        pieces = pieces + [grid.flip(v, bit) for v in pieces]
    query = (mm(flat_low, params["q"]) + params["q_bias"]).astype(BF)
    if hooks is None:
        mixed, lse = attend(query, pieces, mask)
    else:
        pairs = query.shape[1] // 128
        part = attend(query, pieces, mask, 0, pairs // 2)
        query, part, waiting = hooks[0](query, part)
        mixed, lse = attend(query, pieces, mask, pairs // 2, pairs - pairs // 2, part)
        mixed, more, waiting = hooks[1](mixed, waiting)
        params.update(more)
    joined = hidden + mm(mixed, params["out"]) + params["out_bias"]
    first = normalize(joined, params["first_gain"], params["first_shift"])
    first_low = first.astype(BF)
    if hooks is not None:
        first_low, waiting = hooks[2](first_low, waiting)
    inner = mm(first_low, params["up"]) + params["up_bias"]
    act_low = activate(inner).astype(BF)
    if hooks is not None:
        act_low, more = hooks[3](act_low, waiting)
        params.update(more)
    summed = first + mm(act_low, params["down"]) + params["down_bias"]
    result = normalize(summed, params["second_gain"], params["second_shift"])
    return result, (flat_low, query, pieces, mixed, lse, joined, first_low, inner, act_low, summed)


class Backward:
    def __init__(self, grid, group_bits, saved, params, mask):
        self.grid, self.group_bits, self.params, self.mask = grid, group_bits, params, mask
        (
            self.flat_low,
            self.query,
            self.pieces,
            self.mixed,
            self.lse,
            self.joined,
            self.first_low,
            self.inner,
            self.act_low,
            self.summed,
        ) = saved

    def top(self, grad_out):
        p = self.params
        _, back = jax.vjp(normalize, self.summed, p["second_gain"], p["second_shift"])
        self.d_summed, self.d_second_gain, self.d_second_shift = back(grad_out)
        self.d_down = self.d_summed.astype(BF)

    def hidden_units(self):
        d_act = mm_back(self.d_down, self.params["down"])
        _, act_back = jax.vjp(activate, self.inner)
        self.d_inner = act_back(d_act)[0].astype(BF)

    def middle(self):
        p = self.params
        d_first = self.d_summed + mm_back(self.d_inner, p["up"])
        _, back = jax.vjp(normalize, self.joined, p["first_gain"], p["first_shift"])
        self.d_joined, self.d_first_gain, self.d_first_shift = back(d_first)
        self.d_branch = self.d_joined.astype(BF)

    def attention(self, begin, pairs):
        d_query, d_keyed = attend_back(
            self.query, self.d_mixed, self.mixed, self.lse, self.pieces, self.mask, begin, pairs
        )
        for bit in reversed(self.group_bits):
            half = len(d_keyed) // 2
            sent = [self.grid.flip(v, bit) for v in d_keyed[half:]]
            d_keyed = [
                (mine.astype(F32) + got.astype(F32)).astype(BF)
                for mine, got in zip(d_keyed[:half], sent)
            ]
        return d_query, d_keyed[0]

    def collect(self, parts):
        self.d_query = side_by_side([q for q, _ in parts], 1)
        self.d_keyed = jnp.concatenate([kv[i] for i in range(2) for _, kv in parts], 1)

    def start(self):
        return (
            self.d_joined
            + mm_back(self.d_query, self.params["q"])
            + mm_back(self.d_keyed, self.params["kv"])
        )

    def vectors(self):
        model = self.d_query.shape[1]
        rows = (
            column_sum(self.d_query),
            column_sum(self.d_keyed[:, model:]),
            column_sum(self.d_branch),
            self.d_first_gain,
            self.d_first_shift,
            column_sum(self.d_down),
            self.d_second_gain,
            self.d_second_shift,
        )
        return rows, column_sum(self.d_inner)


def local(n_dp, n_ctx, tokens, lengths, teacher, *shards):
    (
        query_weight,
        query_bias,
        key_weight,
        value_weight,
        value_bias,
        out_weight,
        out_bias,
        first_gain,
        first_shift,
        up_weight,
        up_bias,
        down_weight,
        down_bias,
        second_gain,
        second_shift,
    ) = shards
    grid = Grid(n_dp, n_ctx)
    width, seqs, model = tokens.shape
    inner_width = up_weight.shape[1]
    rows = query_weight.shape[0]
    block = rows * n_ctx

    spread = n_ctx // (2 * seqs)
    mine = grid.ctx // spread
    member = grid.core * spread + grid.ctx % spread
    group_bits = [1 << i for i in range(spread.bit_length() - 1)] + [grid.core_bit]

    def route(turn):
        pairs = []
        for pair in range(n_dp // 2):
            for core in range(2):
                for at in range(n_ctx):
                    seq = core * seqs + (at + turn) % seqs
                    to = at // seqs
                    there = (pair * 2 + to // spread) * n_ctx + seq * spread + to % spread
                    pairs.append(((pair * 2 + core) * n_ctx + at, there))
        return pairs

    def to_group(values, turn):
        value = lax.dynamic_index_in_dim(values, (grid.ctx + turn) % seqs, 1, keepdims=False)
        return lax.ppermute(value, AXES, route(turn))

    def to_groups(values):
        return jnp.concatenate([to_group(values, turn) for turn in range(seqs)], 0)

    def from_groups(values):
        got = [
            lax.ppermute(
                values[turn * width : (turn + 1) * width],
                AXES,
                [(there, here) for here, there in route(turn)],
            )
            for turn in range(seqs)
        ]
        return jnp.stack(
            [
                functools.reduce(
                    lambda a, t: jnp.where((grid.ctx + t) % seqs == seq, got[t], a),
                    range(1, seqs),
                    got[0],
                )
                for seq in range(seqs)
            ],
            1,
        )

    turns = list(reversed(grid.ctx_bits))
    vectors = (
        query_bias,
        value_bias,
        out_bias,
        first_gain,
        first_shift,
        down_bias,
        second_gain,
        second_shift,
    )
    one = [jnp.concatenate([query_weight, key_weight, value_weight], 1)]
    small = [
        jnp.concatenate(
            [jnp.stack(vectors, 0).T, up_bias.reshape(rows, -1), jnp.zeros((rows, 116), BF)], 1
        )
    ]
    two, three = [jnp.concatenate([out_weight, up_weight], 1)], [down_weight]
    last = len(turns) - 1
    got_two = None
    for i, turn in enumerate(turns):
        got = [grid.flip(side_by_side(v), turn) for v in (one, small)]
        if got_two is not None:
            two = join_ctx(grid, two, got_two, turns[i - 2])
        got_two = grid.flip(side_by_side(two), turns[i - 1]) if i else None
        got, got_two, two, tokens = meet(got, got_two, two, tokens)
        one, small = join_ctx(grid, one, got[0], turn), join_ctx(grid, small, got[1], turn)
    if got_two is not None:
        two = join_ctx(grid, two, got_two, turns[last - 1])
    first = Gather(grid, jnp.concatenate([side_by_side(one), side_by_side(small)], 1))
    got, start, two, tokens = meet(
        first.first(), [to_group(tokens, turn) for turn in range(seqs - 1)], two, tokens
    )
    more, crossed = first.second(*got)
    got_two = grid.flip(side_by_side(two), turns[last])
    more, crossed, start, got_two, two, three = meet(
        more, crossed, start + [to_group(tokens, seqs - 1)], got_two, two, three
    )
    second = Gather(grid, side_by_side(join_ctx(grid, two, got_two, turns[last])))
    second_got = second.first()
    for turn in turns[:-1]:
        three = join_ctx(grid, three, grid.flip(side_by_side(three), turn), turn)
    start = jnp.concatenate(start, 0)
    whole_q, whole_kv, whole_small = assemble(
        grid,
        first.finish(more, crossed),
        block,
        [
            (0, model, 0, 0, block, 0),
            (model, 2 * model, 1, 0, block, 0),
            (3 * model, 128, 2, 0, block, 0),
        ],
        [(model, model), (model, 2 * model), (model, 128)],
    )
    flat_small = whole_small[:, :12].astype(F32)
    by_vector = flat_small[:, :8].T
    params = {
        "q": whole_q,
        "kv": whole_kv,
        "q_bias": by_vector[0],
        "kv_bias": jnp.concatenate([jnp.zeros((model,), F32), by_vector[1]]),
        "out_bias": by_vector[2],
        "first_gain": by_vector[3],
        "first_shift": by_vector[4],
        "down_bias": by_vector[5],
        "second_gain": by_vector[6],
        "second_shift": by_vector[7],
        "up_bias": flat_small[:, 8:12].reshape(inner_width),
    }

    theirs = grid.flip(lengths, grid.core_bit)
    length = jnp.where(mine // seqs == grid.core, lengths[mine % seqs], theirs[mine % seqs])

    def slots_of(who):
        place = jnp.arange(width, dtype=jnp.int32)
        return jnp.concatenate(
            [width * (seqs * who + (mine + turn) % seqs) + place for turn in range(seqs)]
        )

    live = (slots_of(member) < length).astype(F32)[:, None]
    relative = [0]
    for bit in group_bits:
        relative = relative + [r ^ (spread if bit == grid.core_bit else bit) for r in relative]
    excluded = jnp.stack([jnp.where(slots_of(member ^ r) < length, 0.0, MASKED) for r in relative])
    mask = jnp.where(jnp.arange(128) % HD == 0, excluded[:, :, None], 0.0).astype(BF)

    def middle_of_attention(query, part):
        query, part, got, parts = meet(query, part, second_got, three)
        state = second.second(*got)
        return query, part, (state, parts, grid.flip(side_by_side(parts), turns[last]))

    def after_attention(mixed, waiting):
        mixed, (more, crossed), parts, got = meet(mixed, *waiting)
        third = Gather(grid, side_by_side(join_ctx(grid, parts, got, turns[last])))
        got = third.first()
        whole_out, whole_up = assemble(
            grid,
            second.finish(more, crossed),
            block,
            [(0, model, 0, 0, block, 0), (model, inner_width, 1, 0, block, 0)],
            [(model, model), (model, inner_width)],
        )
        return mixed, {"out": whole_out, "up": whole_up}, (third, got)

    def before_up(first_low, waiting):
        third, got = waiting
        first_low, got = meet(first_low, got)
        return first_low, (third, third.second(*got))

    def after_up(act_low, waiting):
        third, state = waiting
        act_low, (more, crossed) = meet(act_low, state)
        tall = third.part.shape[0]
        (whole_down,) = assemble(
            grid,
            third.finish(more, crossed),
            tall,
            [(0, model, 0, 0, tall, 0)],
            [(inner_width, model)],
        )
        return act_low, {"down": whole_down}

    hooks = (middle_of_attention, after_attention, before_up, after_up)
    middle, first_saved = forward_layer(
        grid, group_bits, start.astype(F32), params, mask, hooks
    )
    target = to_groups(after(teacher, middle))
    result, second_saved = forward_layer(grid, group_bits, middle, params, mask)
    layer_out = from_groups(result.astype(BF))
    diff = (result - target.astype(F32)) * live
    error = jnp.sum(diff * diff)

    pairs = model // 128
    b = Backward(grid, group_bits, second_saved, params, mask)
    b.top(diff)
    b.hidden_units()
    b.middle()
    b.d_mixed = mm_back(b.d_branch, params["out"]).astype(BF)
    b.collect([b.attention(0, pairs)])
    d_middle = b.start()

    a = Backward(grid, group_bits, first_saved, params, mask)
    a.top(d_middle)
    downs = grads(grid, [b.act_low, a.act_low], [b.d_down, a.d_down])
    reduce_down, reduce_up, reduce_rest = Reduce(grid), Reduce(grid), Reduce(grid)
    reduce_down.add(*downs)
    a.d_down = after(a.d_down, downs)
    a.hidden_units()
    ups = grads(grid, [b.first_low, a.first_low], [b.d_inner, a.d_inner])
    reduce_up.add(*ups)
    reduce_down.first(ups)
    a.d_inner = after(a.d_inner, ups)
    a.middle()
    outs = grads(grid, [b.mixed, a.mixed], [b.d_branch, a.d_branch])
    reduce_up.add(*outs)
    a.d_mixed = mm_back(after(a.d_branch, outs, reduce_down.sent()), params["out"]).astype(BF)
    part_one = a.attention(0, pairs // 2)
    reduce_down.second(part_one[0])
    reduce_up.first(part_one[0])
    a.d_mixed = after(a.d_mixed, part_one, reduce_down.sent(), reduce_up.sent())
    reduce_down.third(reduce_up.halves)
    part_two = a.attention(pairs // 2, pairs - pairs // 2)
    a.collect([part_one, part_two])
    lefts = [b.flat_low, a.flat_low]
    rest_q = grads(grid, lefts, [b.d_query, a.d_query])
    reduce_rest.add(*rest_q)
    reduce_up.second(rest_q)
    rest_kv = grads(grid, lefts, [b.d_keyed, a.d_keyed])
    reduce_rest.add(*rest_kv)
    reduce_down.fourth(rest_kv)
    rows_b, wide_b = b.vectors()
    rows_a, wide_a = a.vectors()
    stacked = (jnp.concatenate(rows_b) + jnp.concatenate(rows_a)).reshape(8, model)
    number = jnp.sum(live)
    whole = [(v, v.astype(BF).astype(F32)) for v in (error, number)]
    here = (jnp.arange(grid.n) == grid.lin)[None, :]
    marks = [jnp.where(here, v, 0.0) for full, low in whole for v in (low, full - low)]
    spare = -(12 + 4 * grid.n) % 128
    marks = jnp.concatenate(marks + [jnp.zeros((1, spare), F32)], 1)
    small = jnp.concatenate(
        [
            stacked.T,
            (wide_b + wide_a).reshape(model, -1),
            jnp.broadcast_to(marks, (model, marks.shape[1])),
        ],
        1,
    ).reshape(n_dp // 2, 2, block, -1)
    pick = functools.partial(lax.dynamic_index_in_dim, axis=1, keepdims=False)
    reduce_rest.add(pick(small, 1 - grid.core).astype(BF), pick(small, grid.core))
    a.d_query = after(a.d_query, rest_kv)
    d_start = a.start()
    grad_tokens = from_groups(d_start.astype(BF))
    reduce_rest.first(d_start)
    reduce_up.third(reduce_rest.sent())
    reduce_rest.second()
    reduce_up.fourth(reduce_rest.sent())
    reduce_rest.third()
    grad_down = reduce_down.finish_value()
    grad_out_up = reduce_up.finish_value()
    grad_rest = reduce_rest.finish_value()
    grad_small = grad_rest[:, 3 * model :]
    sums = jnp.sum(grad_small[:1, 12 : 12 + 4 * grid.n].reshape(4, grid.n), axis=1)
    loss = (sums[0] + sums[1]) / ((sums[2] + sums[3]) * model)
    vector = [grad_small[:, i] for i in range(8)]
    return (
        layer_out,
        loss,
        grad_tokens,
        grad_rest[:, :model],
        vector[0],
        grad_rest[:, model : 2 * model],
        grad_rest[:, 2 * model : 3 * model],
        vector[1],
        grad_out_up[:, inner_width:],
        vector[2],
        vector[3],
        vector[4],
        grad_out_up[:, :inner_width],
        grad_small[:, 8:12].reshape(-1),
        grad_down,
        vector[5],
        vector[6],
        vector[7],
    )


def solution(mesh):
    matrix, vector = P(AXES, None), P(AXES)
    states = P("ctx", "dp", None)
    params = (
        matrix,
        vector,
        matrix,
        matrix,
        vector,
        matrix,
        vector,
        vector,
        vector,
        matrix,
        vector,
        matrix,
        vector,
        vector,
        vector,
    )
    return jax.shard_map(
        functools.partial(local, mesh.shape["dp"], mesh.shape["ctx"]),
        mesh=mesh,
        in_specs=(states, P("dp"), states) + params,
        out_specs=(states, P(), states) + params,
        check_vma=False,
    )
```

time: 554 us -> 477 us (0.86)
  Pallas kernels: 79.6 us -> 121 us
  waiting for transfers between devices: 123 us -> 87.3 us
  local copies, waits for them, and re-layouts: 90.1 us -> 60.7 us
  matrix products: 103 us -> 75.9 us
  starting transfers between devices: 80.3 us -> 57.7 us
    ppermute x56 -> x62, waiting for transfers between devices: 110 us -> 59.6 us  [flip(): return lax.ppermute(value, AXES, [(i, i ^ mask) for i in range(self.n)])]
    dot_general x8 -> x0, matrix products: 43 us -> none  [mm_rows(): lax.dot_general(left, right, (((0,), (0,)), ((), ())), preferred_element_...]
    pallas_call x2 -> x8, Pallas kernels: 28.4 us -> 66.4 us  [the longest x5 35.9 us: grads(): pl.pallas_call(functools.partial(grads_kernel, count, top, whole), out_sh...]
    ppermute x56 -> x62, starting transfers between devices: 61.6 us -> 41.5 us  [flip(): return lax.ppermute(value, AXES, [(i, i ^ mask) for i in range(self.n)])]
    ppermute x4, waiting for transfers between devices: 0.01 us -> 19.8 us  [to_group(): return lax.ppermute(value, AXES, route(turn))]
    add x9 -> x2, local copies, waits for them, and re-layouts: 12.8 us -> 1.16 us  [the longest x1 1.16 us: local(): wide_b + wide_a]
    concatenate x8 -> x20, other arithmetic: 1.06 us -> 12 us  [the longest x3 3.7 us: second(): jnp.concatenate(moved, 0)]
    dot_general x12 -> x10, matrix products: 32.7 us -> 41.2 us  [mm_back(): lax.dot_general(left, right, (((1,), (1,)), ((), ())), preferred_element_...]
  transfers between devices with their start and end apart: 64 -> 70, of which waited for: 20 -> 19; matrix products, arithmetic and copies ran while one was open for 34% -> 28% of each run, Pallas kernels for 13% -> 18%
where the time goes in v2:
time: 477 us; the launch traced here: 470 us
  Pallas kernels  121 us (25%)
  waiting for transfers between devices  87.3 us (18%)
  matrix products  75.9 us (16%)
  local copies, waits for them, and re-layouts  60.7 us (13%)
  starting transfers between devices  57.7 us (12%)
  other arithmetic  55.7 us (12%)
  between operations  11.2 us (2%)
    ppermute x62, waiting for transfers between devices, flip(): return lax.ppermute(value, AXES, [(i, i ^ mask) for i in range(self.n)])  59.6 us
    ppermute x62, starting transfers between devices, flip(): return lax.ppermute(value, AXES, [(i, i ^ mask) for i in range(self.n)])  41.5 us
    dot_general x10, matrix products, mm_back(): lax.dot_general(left, right, (((1,), (1,)), ((), ())), preferred_element_...  41.2 us
    pallas_call x3, Pallas kernels, attend_back(): pl.pallas_call(functools.partial(attend_back_kernel, count, HD ** (-0.5))...  40.5 us
    pallas_call x5, Pallas kernels, grads(): pl.pallas_call(functools.partial(grads_kernel, count, top, whole), out_sh...  35.9 us
    dot_general x10, matrix products, mm(): return jnp.dot(left, right, preferred_element_type=F32)  34.7 us
    pallas_call x3, Pallas kernels, attend(): pl.pallas_call(kernel, grid=(pairs,), in_specs=[at(0), pl.BlockSpec((coun...  30.5 us
    unnamed x284, local copies, waits for them, and re-layouts  24.1 us
  transfers between devices with their start and end apart: 70, of which 19 were waited for; matrix products, arithmetic and copies ran while one was open for 28% of the time, Pallas kernels for 18%

profile of v2, /device:TPU:1, one launch (start us, length us, event | category | flops | bytes accessed | tf_op | source)
XLA Modules:
  0.0 469.6 jit_solution(17632849567652033564)
XLA Ops:
  17.6 8.3 %collective-permute-done.3 = bf16[48,128]{1,0:T(8,128)(2,1)S(1)} collective-permute-done((bf16[48,128]{1,0:T(8,128)(2,1)S(1)}, bf16[48,128]{1,0:T(8,128)(2,1)S(1)}, u32[]{:S(2)}, u32[]{:S(2)}) %collective-permute-start.3) | collective-permute-done | bytes 12320 | tf_op jit(solution)/shard_map/ppermute | solution.py:57
  34.0 11.6 %collective-permute-done.8 = bf16[256,768]{1,0:T(8,128)(2,1)S(1)} collective-permute-done((bf16[256,768]{1,0:T(8,128)(2,1)S(1)}, bf16[256,768]{1,0:T(8,128)(2,1)S(1)}, u32[]{:S(2)}, u32[]{:S(2)}) %collective-permute-start.8) | collective-permute-done | bytes 393248 | tf_op jit(solution)/shard_map/ppermute | solution.py:561
  53.3 5.5 %collective-permute-done.9.refs_3_ = bf16[96,1152]{1,0:T(8,128)(2,1)S(1)} collective-permute-done((bf16[96,1152]{1,0:T(8,128)(2,1)S(1)}, bf16[96,1152]{1,0:T(8,128)(2,1)S(1)}, u32[]{:S(2)}, u32[]{:S(2)}) %collective-permute-start.9) | collective-permute-done | bytes 221216 | tf_op jit(solution)/shard_map/ppermute | solution.py:57
  59.3 8.2 %collective-permute-done.12 = bf16[256,768]{1,0:T(8,128)(2,1)S(1)} collective-permute-done((bf16[256,768]{1,0:T(8,128)(2,1)S(1)}, bf16[256,768]{1,0:T(8,128)(2,1)S(1)}, u32[]{:S(2)}, u32[]{:S(2)}) %collective-permute-start.12) | collective-permute-done | bytes 393248 | tf_op jit(solution)/shard_map/ppermute | solution.py:561
  85.3 8.7 %collective-permute-done.21 = bf16[96,768]{1,0:T(8,128)(2,1)S(1)} collective-permute-done((bf16[96,768]{1,0:T(8,128)(2,1)S(1)}, bf16[96,768]{1,0:T(8,128)(2,1)S(1)}, u32[]{:S(2)}, u32[]{:S(2)}) %collective-permute-start.21) | collective-permute-done | bytes 147488 | tf_op jit(solution)/shard_map/ppermute | solution.py:57
  97.0 8.3 %attend.3 = (bf16[512,768]{1,0:T(8,128)(2,1)}, f32[6,8,512]{2,1,0:T(8,128)}) custom-call(bf16[512,768]{1,0:T(8,128)(2,1)} %add_convert_fusion.4.refs_0_.q_ref, bf16[2,512,128]{2,1,0:T(8,128)(2,1)} %select_convert_fusion.refs_1_.mask_ref, bf16[512,1536]{1,0:T(8,128)(2,1)} %copy-done, bf16[512,1536]{1,0:T(8,128)(2,1)} %copy-done.1, bf16[512,1536]{1,0:T(8,128)(2,1)} %copy-done, ...), custom_call_target="tpu_custom_call" | custom-call | tf_op jit(solution)/shard_map/attend/pallas_call | solution.py:332
  109.5 8.1 %attend.4 = (bf16[512,768]{1,0:T(8,128)(2,1)}, f32[6,8,512]{2,1,0:T(8,128)}) custom-call(bf16[512,768]{1,0:T(8,128)(2,1)} %add_convert_fusion.4.refs_0_.q_ref, bf16[2,512,128]{2,1,0:T(8,128)(2,1)} %select_convert_fusion.refs_1_.mask_ref, bf16[512,1536]{1,0:T(8,128)(2,1)} %copy-done, ...), custom_call_target="tpu_custom_call", output_to_operand_aliasing={{0}: (6, {}), {1}: (7, {})} | custom-call | tf_op jit(solution)/shard_map/attend/pallas_call | solution.py:332
  142.1 9.1 %multiply_convert_fusion.1 = (bf16[512,3072]{1,0:T(8,128)(2,1)}, f32[512,3072]{1,0:T(8,128)}) fusion(f32[3072]{0:T(1024)S(1)} %add.597, bf16[512,768]{1,0:T(8,128)(2,1)S(1)} %fusion.16.refs_1_, bf16[768,3072]{1,0:T(8,128)(2,1)} %get-tuple-element.183), kind=kOutput, calls=%fused_computation.21 | convolution fusion | flops 2431647744 | bytes 14954496 | tf_op jit(solution)/shard_map/dot_general | solution.py:21
  159.8 6.0 %fusion.65 = (f32[512]{0:T(512)S(1)}, f32[512,768]{1,0:T(8,128)S(1)}) fusion(f32[768]{0:T(1024)S(1)} %copy-done.104, bf16[512,3072]{1,0:T(8,128)(2,1)} %get-tuple-element.187.refs_1_, bf16[3072,768]{1,0:T(8,128)(2,1)} %assemble.5, f32[768]{0:T(1024)S(1)} %get-tuple-element.312, f32[768]{0:T(1024)S(1)} %get-tuple-element.313, f32[512]{0:T(512)S(1)} %fusion.37, ...), kind=kOutput, calls=%fused_computation.298 | convolution fusion | flops 2418671104 | bytes 11025408 | tf_op jit(solution)/shard_map/dot_general | solution.py:21
  178.5 14.1 %attend.5 = (bf16[512,768]{1,0:T(8,128)(2,1)}, f32[6,8,512]{2,1,0:T(8,128)}) custom-call(bf16[512,768]{1,0:T(8,128)(2,1)} %add_convert_fusion.3.refs_0_.q_ref, bf16[2,512,128]{2,1,0:T(8,128)(2,1)} %select_convert_fusion.refs_1_.mask_ref, bf16[512,1536]{1,0:T(8,128)(2,1)} %copy-done.2, bf16[512,1536]{1,0:T(8,128)(2,1)} %copy-done.3, ...), custom_call_target="tpu_custom_call" | custom-call | tf_op jit(solution)/shard_map/attend/pallas_call | solution.py:332
  195.7 6.1 %multiply_convert_fusion = (bf16[512,3072]{1,0:T(8,128)(2,1)S(1)}, f32[512,3072]{1,0:T(8,128)S(1)}) fusion(f32[3072]{0:T(1024)S(1)} %add.597, bf16[512,768]{1,0:T(8,128)(2,1)S(1)} %fusion.17.refs_0_, bf16[768,3072]{1,0:T(8,128)(2,1)} %get-tuple-element.183), kind=kOutput, calls=%fused_computation.20 | convolution fusion | flops 2431647744 | bytes 14954496 | tf_op jit(solution)/shard_map/dot_general | solution.py:21
  208.6 7.2 %convert_reduce_fusion.1 = (f32[3072]{0:T(1024)}, bf16[512,3072]{1,0:T(8,128)(2,1)S(1)}) fusion(f32[512,3072]{1,0:T(8,128)S(1)} %get-tuple-element.425, f32[3072]{0:T(1024)S(1)} %add.597, bf16[512,768]{1,0:T(8,128)(2,1)S(1)} %get-tuple-element.332.refs_2_, bf16[3072,768]{1,0:T(8,128)(2,1)S(1)} %bitcast.176), kind=kOutput, calls=%fused_computation.19 | convolution fusion | flops 2452091904 | bytes 14966784 | tf_op jit(solution)/shard_map/dot_general | solution.py:29
  224.0 19.0 %attend_back.3 = (bf16[512,768]{1,0:T(8,128)(2,1)}, bf16[2,512,768]{2,1,0:T(8,128)(2,1)}, bf16[2,512,768]{2,1,0:T(8,128)(2,1)}) custom-call(bf16[512,768]{1,0:T(8,128)(2,1)} %add_convert_fusion.3.refs_0_.q_ref, bf16[512,768]{1,0:T(8,128)(2,1)} %convolution_convert_fusion.1.do_ref, bf16[512,768]{1,0:T(8,128)(2,1)} %get-tuple-element.194.o_ref.refs_0_, ...), custom_call_target="tpu_custom_call" | custom-call | tf_op jit(solution)/shard_map/attend_back/pallas_call | solution.py:397
  261.0 7.9 %collective-permute-done.38 = bf16[256,768]{1,0:T(8,128)(2,1)} collective-permute-done((bf16[256,768]{1,0:T(8,128)(2,1)}, bf16[256,768]{1,0:T(8,128)(2,1)}, u32[]{:S(2)}, u32[]{:S(2)}) %collective-permute-start.38) | collective-permute-done | bytes 393248 | tf_op jit(solution)/shard_map/ppermute | solution.py:568
  280.0 10.5 %grads.5 = (bf16[4,384,768]{2,1,0:T(8,128)(2,1)}, f32[4,384,768]{2,1,0:T(8,128)}) custom-call(s32[1]{0:T(128)} %bitcast.21.core, bf16[512,3072]{1,0:T(8,128)(2,1)} %copy-done.30, bf16[512,3072]{1,0:T(8,128)(2,1)} %get-tuple-element.187.refs_1_, bf16[512,768]{1,0:T(8,128)(2,1)} %copy-done.40, bf16[512,768]{1,0:T(8,128)(2,1)} %add_convert_fusion.6.refs_3_), custom_call_target="tpu_custom_call" | custom-call | tf_op jit(solution)/shard_map/grads/pallas_call | solution.py:197
  290.5 9.9 %fusion.6.refs_3_ = bf16[512,3072]{1,0:T(8,128)(2,1)} fusion(f32[512,3072]{1,0:T(8,128)} %get-tuple-element.419, f32[3072]{0:T(1024)S(1)} %copy-done.94, bf16[512,768]{1,0:T(8,128)(2,1)S(1)} %copy-done.9, bf16[3072,768]{1,0:T(8,128)(2,1)} %assemble.5), kind=kOutput, calls=%fused_computation.10 | convolution fusion | flops 2448949248 | bytes 14954496 | tf_op jit(solution)/shard_map/dot_general | solution.py:29
  300.4 9.9 %grads.6 = (bf16[4,96,3072]{2,1,0:T(8,128)(2,1)}, f32[4,96,3072]{2,1,0:T(8,128)}) custom-call(s32[1]{0:T(128)} %bitcast.21.core, bf16[512,768]{1,0:T(8,128)(2,1)} %copy-done.39, bf16[512,768]{1,0:T(8,128)(2,1)} %copy-done.38, bf16[512,3072]{1,0:T(8,128)(2,1)} %copy-done.31, bf16[512,3072]{1,0:T(8,128)(2,1)} %fusion.6.refs_3_), custom_call_target="tpu_custom_call" | custom-call | tf_op jit(solution)/shard_map/grads/pallas_call | solution.py:197
  310.8 6.5 %multiply_reduce_fusion.2 = (f32[768]{0:T(1024)}, f32[512]{0:T(512)S(1)}, f32[768]{0:T(1024)}, f32[512,768]{1,0:T(8,128)S(1)}) fusion(f32[512,768]{1,0:T(8,128)S(1)} %get-tuple-element.349, f32[512]{0:T(512)S(1)} %copy-done.84, f32[512]{0:T(512)S(1)} %copy-done.78, f32[768]{0:T(1024)S(1)} %get-tuple-element.313, bf16[512,3072]{1,0:T(8,128)(2,1)S(1)} %copy-done.4, ...), kind=kOutput, calls=%fused_computation.42 | convolution fusion | flops 2419849216 | bytes 12600320 | tf_op jit(solution)/shard_map/dot_general | solution.py:29
  336.9 10.9 %attend_back.4 = (bf16[512,384]{1,0:T(8,128)(2,1)}, bf16[2,512,384]{2,1,0:T(8,128)(2,1)}, bf16[2,512,384]{2,1,0:T(8,128)(2,1)}) custom-call(bf16[512,768]{1,0:T(8,128)(2,1)} %add_convert_fusion.4.refs_0_.q_ref, bf16[512,768]{1,0:T(8,128)(2,1)} %convolution_convert_fusion.do_ref, bf16[512,768]{1,0:T(8,128)(2,1)} %get-tuple-element.171.refs_1_.o_ref, ...), custom_call_target="tpu_custom_call" | custom-call | tf_op jit(solution)/shard_map/attend_back/pallas_call | solution.py:397
  363.6 10.7 %attend_back.5 = (bf16[512,384]{1,0:T(8,128)(2,1)}, bf16[2,512,384]{2,1,0:T(8,128)(2,1)}, bf16[2,512,384]{2,1,0:T(8,128)(2,1)}) custom-call(bf16[512,768]{1,0:T(8,128)(2,1)} %add_convert_fusion.4.refs_0_.q_ref, bf16[512,768]{1,0:T(8,128)(2,1)} %convolution_convert_fusion.do_ref, bf16[512,768]{1,0:T(8,128)(2,1)} %get-tuple-element.171.refs_1_.o_ref, ...), custom_call_target="tpu_custom_call" | custom-call | tf_op jit(solution)/shard_map/attend_back/pallas_call | solution.py:397
  393.2 6.4 %grads.9 = (bf16[4,96,1536]{2,1,0:T(8,128)(2,1)}, f32[4,96,1536]{2,1,0:T(8,128)}) custom-call(s32[1]{0:T(128)} %bitcast.21.core, bf16[512,768]{1,0:T(8,128)(2,1)} %copy-done.8, bf16[512,768]{1,0:T(8,128)(2,1)} %copy-done.15, bf16[512,1536]{1,0:T(8,128)(2,1)} %pad_maximum_fusion.2.refs_2_, bf16[512,1536]{1,0:T(8,128)(2,1)} %pad_maximum_fusion.3.refs_3_), custom_call_target="tpu_custom_call" | custom-call | tf_op jit(solution)/shard_map/grads/pallas_call | solution.py:197
  427.2 5.8 %collective-permute-done.53 = bf16[2,96,1280]{2,1,0:T(8,128)(2,1)S(1)} collective-permute-done((bf16[2,96,1280]{2,1,0:T(8,128)(2,1)S(1)}, bf16[2,96,1280]{2,1,0:T(8,128)(2,1)S(1)}, u32[]{:S(2)}, u32[]{:S(2)}) %collective-permute-start.53) | collective-permute-done | bytes 491552 | tf_op jit(solution)/shard_map/ppermute | solution.py:57
  449.1 5.4 %collective-permute-done.56 = bf16[2,24,2560]{2,1,0:T(8,128)(2,1)S(1)} collective-permute-done((bf16[2,24,2560]{2,1,0:T(8,128)(2,1)S(1)}, bf16[2,24,2560]{2,1,0:T(8,128)(2,1)S(1)}, u32[]{:S(2)}, u32[]{:S(2)}) %collective-permute-start.56) | collective-permute-done | bytes 245792 | tf_op jit(solution)/shard_map/ppermute | solution.py:57
  456.2 6.3 %collective-permute-done.57 = bf16[1,24,2560]{2,1,0:T(8,128)(2,1)S(1)} collective-permute-done((bf16[1,24,2560]{2,1,0:T(8,128)(2,1)S(1)}, bf16[1,24,2560]{2,1,0:T(8,128)(2,1)S(1)}, u32[]{:S(2)}, u32[]{:S(2)}) %collective-permute-start.57) | collective-permute-done | bytes 122912 | tf_op jit(solution)/shard_map/ppermute | solution.py:57
  (627 shorter events, 247.8 us)
Async XLA Ops:
  7.9 42.8 %collective-permute-start.16 = (s32[2]{0:T(128)}, s32[2]{0:T(128)S(1)}, u32[]{:S(2)}, u32[]{:S(2)}) collective-permute-start(s32[2]{0:T(128)} %param.19), channel_id=1, source_target_pairs={{0,4},{1,5},{2,6},{3,7},{4,0},{5,1},{6,2},{7,3},{8,12},{9,13},{10,... | collective-permute-start | bytes 32 | tf_op jit(solution)/shard_map/ppermute | solution.py:57
  26.7 18.9 %collective-permute-start.5 = (bf16[96,2432]{1,0:T(8,128)(2,1)S(1)}, bf16[96,2432]{1,0:T(8,128)(2,1)S(1)}, u32[]{:S(2)}, u32[]{:S(2)}) collective-permute-start(bf16[96,2432]{1,0:T(8,128)(2,1)S(1)} %maximum_maximum_fusion.1.refs_0_), channel_id=1, source_target_pairs={{0,8},{1,9},{2,10},{3,11},{4,12},{5,13},{6,14},{7,15},{8,0},{9,1},... | collective-permute-start | bytes 1400840 | tf_op jit(solution)/shard_map/ppermute | solution.py:57
  47.5 19.9 %collective-permute-start.11 = (bf16[192,2432]{1,0:T(8,128)(2,1)}, bf16[192,2432]{1,0:T(8,128)(2,1)}, u32[]{:S(2)}, u32[]{:S(2)}) collective-permute-start(bf16[192,2432]{1,0:T(8,128)(2,1)} %pad_maximum_fusion.9), channel_id=1, source_target_pairs={{0,4},{1,5},{2,6},{3,7},{4,0},{5,1},{6,2},{7,3},{8,12},{9,13},{10,... | collective-permute-start | bytes 2801672 | tf_op jit(solution)/shard_map/ppermute | solution.py:57
  48.5 19.0 %collective-permute-start.12 = (bf16[256,768]{1,0:T(8,128)(2,1)S(1)}, bf16[256,768]{1,0:T(8,128)(2,1)S(1)}, u32[]{:S(2)}, u32[]{:S(2)}) collective-permute-start(bf16[256,768]{1,0:T(8,128)(2,1)S(1)} %dynamic-slice_bitcast_fusion.4), channel_id=1, source_target_pairs={{0,1},{1,0},{2,5},{3,4},{4,3},{5,2},{6,7},{7,6},{8,9},{9,8},{10,13... | collective-permute-start | bytes 1179656 | tf_op jit(solution)/shard_map/ppermute | solution.py:561
  82.9 22.4 %collective-permute-start.18 = (bf16[96,3840]{1,0:T(8,128)(2,1)S(1)}, bf16[96,3840]{1,0:T(8,128)(2,1)S(1)}, u32[]{:S(2)}, u32[]{:S(2)}) collective-permute-start(bf16[96,3840]{1,0:T(8,128)(2,1)S(1)} %pad_maximum_fusion.12.refs_0_), channel_id=1, source_target_pairs={{0,8},{1,9},{2,10},{3,11},{4,12},{5,13},{6,14},{7,15},{8,0},{9,1},... | collective-permute-start | bytes 2211848 | tf_op jit(solution)/shard_map/ppermute | solution.py:57
  83.2 22.1 %collective-permute-start.19 = (bf16[96,3840]{1,0:T(8,128)(2,1)S(1)}, bf16[96,3840]{1,0:T(8,128)(2,1)S(1)}, u32[]{:S(2)}, u32[]{:S(2)}) collective-permute-start(bf16[96,3840]{1,0:T(8,128)(2,1)S(1)} %pad_maximum_fusion.12.refs_0_), channel_id=1, source_target_pairs={{0,16},{1,17},{2,18},{3,19},{4,20},{5,21},{6,22},{7,23},{8,24},{9,... | collective-permute-start | bytes 2211848 | tf_op jit(solution)/shard_map/ppermute | solution.py:57
  83.4 21.9 %collective-permute-start.20 = (bf16[96,3840]{1,0:T(8,128)(2,1)S(1)}, bf16[96,3840]{1,0:T(8,128)(2,1)S(1)}, u32[]{:S(2)}, u32[]{:S(2)}) collective-permute-start(bf16[96,3840]{1,0:T(8,128)(2,1)S(1)} %pad_maximum_fusion.12.refs_0_), channel_id=1, source_target_pairs={{0,4},{1,5},{2,6},{3,7},{4,0},{5,1},{6,2},{7,3},{8,12},{9,13},{10,... | collective-permute-start | bytes 2211848 | tf_op jit(solution)/shard_map/ppermute | solution.py:57
  170.7 34.3 %collective-permute-start.39 = (bf16[256,768]{1,0:T(8,128)(2,1)S(1)}, bf16[256,768]{1,0:T(8,128)(2,1)S(1)}, u32[]{:S(2)}, u32[]{:S(2)}) collective-permute-start(bf16[256,768]{1,0:T(8,128)(2,1)S(1)} %get-tuple-element.373), channel_id=1, source_target_pairs={{0,0},{1,1},{2,4},{3,5},{4,2},{5,3},{6,6},{7,7},{8,8},{9,9},{10,12... | collective-permute-start | bytes 1179656 | tf_op jit(solution)/shard_map/ppermute | solution.py:561
  173.4 31.6 %collective-permute-start.40 = (bf16[256,768]{1,0:T(8,128)(2,1)S(1)}, bf16[256,768]{1,0:T(8,128)(2,1)S(1)}, u32[]{:S(2)}, u32[]{:S(2)}) collective-permute-start(bf16[256,768]{1,0:T(8,128)(2,1)S(1)} %get-tuple-element.374), channel_id=1, source_target_pairs={{0,1},{1,0},{2,5},{3,4},{4,3},{5,2},{6,7},{7,6},{8,9},{9,8},{10,13... | collective-permute-start | bytes 1179656 | tf_op jit(solution)/shard_map/ppermute | solution.py:561
  243.0 28.8 %collective-permute-start.41 = (bf16[2,512,768]{2,1,0:T(8,128)(2,1)}, bf16[2,512,768]{2,1,0:T(8,128)(2,1)}, u32[]{:S(2)}, u32[]{:S(2)}) collective-permute-start(bf16[2,512,768]{2,1,0:T(8,128)(2,1)} %get-tuple-element.199), channel_id=1, source_target_pairs={{0,4},{1,5},{2,6},{3,7},{4,0},{5,1},{6,2},{7,3},{8,12},{9,13},{10,... | collective-permute-start | bytes 4718600 | tf_op jit(solution)/shard_map/ppermute | solution.py:57
  290.5 37.9 %collective-permute-start.42 = (bf16[4,384,768]{2,1,0:T(8,128)(2,1)}, bf16[4,384,768]{2,1,0:T(8,128)(2,1)}, u32[]{:S(2)}, u32[]{:S(2)}) collective-permute-start(bf16[4,384,768]{2,1,0:T(8,128)(2,1)} %get-tuple-element.200), channel_id=1, source_target_pairs={{0,4},{1,5},{2,6},{3,7},{4,0},{5,1},{6,2},{7,3},{8,12},{9,13},{10,... | collective-permute-start | bytes 7077896 | tf_op jit(solution)/shard_map/ppermute | solution.py:57
  310.4 37.4 %collective-permute-start.46 = (bf16[4,96,3072]{2,1,0:T(8,128)(2,1)}, bf16[4,96,3072]{2,1,0:T(8,128)(2,1)}, u32[]{:S(2)}, u32[]{:S(2)}) collective-permute-start(bf16[4,96,3072]{2,1,0:T(8,128)(2,1)} %get-tuple-element.203), channel_id=1, source_target_pairs={{0,4},{1,5},{2,6},{3,7},{4,0},{5,1},{6,2},{7,3},{8,12},{9,13},{10,... | collective-permute-start | bytes 7077896 | tf_op jit(solution)/shard_map/ppermute | solution.py:57
  324.8 22.9 %collective-permute-start.47 = (bf16[4,96,768]{2,1,0:T(8,128)(2,1)}, bf16[4,96,768]{2,1,0:T(8,128)(2,1)}, u32[]{:S(2)}, u32[]{:S(2)}) collective-permute-start(bf16[4,96,768]{2,1,0:T(8,128)(2,1)} %get-tuple-element.206), channel_id=1, source_target_pairs={{0,4},{1,5},{2,6},{3,7},{4,0},{5,1},{6,2},{7,3},{8,12},{9,13},{10,... | collective-permute-start | bytes 1769480 | tf_op jit(solution)/shard_map/ppermute | solution.py:57
  333.3 25.5 %collective-permute-start.45 = (bf16[2,384,384]{2,1,0:T(8,128)(2,1)}, bf16[2,384,384]{2,1,0:T(8,128)(2,1)}, u32[]{:S(2)}, u32[]{:S(2)}) collective-permute-start(bf16[2,384,384]{2,1,0:T(8,128)(2,1)} %fusion.22), channel_id=1, source_target_pairs={{0,16},{1,17},{2,18},{3,19},{4,20},{5,21},{6,22},{7,23},{8,24},{9,... | collective-permute-start | bytes 1769480 | tf_op jit(solution)/shard_map/ppermute | solution.py:57
  334.6 24.2 %collective-permute-start.44 = (bf16[2,384,384]{2,1,0:T(8,128)(2,1)}, bf16[2,384,384]{2,1,0:T(8,128)(2,1)}, u32[]{:S(2)}, u32[]{:S(2)}) collective-permute-start(bf16[2,384,384]{2,1,0:T(8,128)(2,1)} %fusion.21), channel_id=1, source_target_pairs={{0,8},{1,9},{2,10},{3,11},{4,12},{5,13},{6,14},{7,15},{8,0},{9,1},... | collective-permute-start | bytes 1769480 | tf_op jit(solution)/shard_map/ppermute | solution.py:57
  354.8 27.1 %collective-permute-start.61 = (bf16[2,96,1920]{2,1,0:T(8,128)(2,1)}, bf16[2,96,1920]{2,1,0:T(8,128)(2,1)}, u32[]{:S(2)}, u32[]{:S(2)}) collective-permute-start(bf16[2,96,1920]{2,1,0:T(8,128)(2,1)} %fusion.20), channel_id=1, source_target_pairs={{0,16},{1,17},{2,18},{3,19},{4,20},{5,21},{6,22},{7,23},{8,24},{9,... | collective-permute-start | bytes 2211848 | tf_op jit(solution)/shard_map/ppermute | solution.py:57
  357.0 24.9 %collective-permute-start.60 = (bf16[2,96,1920]{2,1,0:T(8,128)(2,1)}, bf16[2,96,1920]{2,1,0:T(8,128)(2,1)}, u32[]{:S(2)}, u32[]{:S(2)}) collective-permute-start(bf16[2,96,1920]{2,1,0:T(8,128)(2,1)} %fusion.19), channel_id=1, source_target_pairs={{0,8},{1,9},{2,10},{3,11},{4,12},{5,13},{6,14},{7,15},{8,0},{9,1},... | collective-permute-start | bytes 2211848 | tf_op jit(solution)/shard_map/ppermute | solution.py:57
  362.5 25.7 %collective-permute-start.66 = (bf16[384,384]{1,0:T(8,128)(2,1)}, bf16[384,384]{1,0:T(8,128)(2,1)S(1)}, u32[]{:S(2)}, u32[]{:S(2)}) collective-permute-start(bf16[384,384]{1,0:T(8,128)(2,1)} %get-tuple-element.435), channel_id=1, source_target_pairs={{0,16},{1,17},{2,18},{3,19},{4,20},{5,21},{6,22},{7,23},{8,24},{9,... | collective-permute-start | bytes 884744 | tf_op jit(solution)/shard_map/ppermute | solution.py:57
  362.9 26.3 %collective-permute-start.67 = (bf16[384,384]{1,0:T(8,128)(2,1)S(1)}, bf16[384,384]{1,0:T(8,128)(2,1)}, u32[]{:S(2)}, u32[]{:S(2)}) collective-permute-start(bf16[384,384]{1,0:T(8,128)(2,1)S(1)} %get-tuple-element.436), channel_id=1, source_target_pairs={{0,8},{1,9},{2,10},{3,11},{4,12},{5,13},{6,14},{7,15},{8,0},{9,1},... | collective-permute-start | bytes 884744 | tf_op jit(solution)/shard_map/ppermute | solution.py:57
  380.7 33.4 %collective-permute-start.48 = (bf16[4,96,768]{2,1,0:T(8,128)(2,1)}, bf16[4,96,768]{2,1,0:T(8,128)(2,1)}, u32[]{:S(2)}, u32[]{:S(2)}) collective-permute-start(bf16[4,96,768]{2,1,0:T(8,128)(2,1)} %get-tuple-element.221), channel_id=1, source_target_pairs={{0,4},{1,5},{2,6},{3,7},{4,0},{5,1},{6,2},{7,3},{8,12},{9,13},{10,... | collective-permute-start | bytes 1769480 | tf_op jit(solution)/shard_map/ppermute | solution.py:57
  386.1 36.2 %collective-permute-start.62 = (bf16[96,1920]{1,0:T(8,128)(2,1)}, bf16[96,1920]{1,0:T(8,128)(2,1)}, u32[]{:S(2)}, u32[]{:S(2)}) collective-permute-start(bf16[96,1920]{1,0:T(8,128)(2,1)} %fusion.25), channel_id=1, source_target_pairs={{0,16},{1,17},{2,18},{3,19},{4,20},{5,21},{6,22},{7,23},{8,24},{9,... | collective-permute-start | bytes 1105928 | tf_op jit(solution)/shard_map/ppermute | solution.py:57
  388.2 35.7 %collective-permute-start.63 = (bf16[96,1920]{1,0:T(8,128)(2,1)}, bf16[96,1920]{1,0:T(8,128)(2,1)}, u32[]{:S(2)}, u32[]{:S(2)}) collective-permute-start(bf16[96,1920]{1,0:T(8,128)(2,1)} %fusion.26), channel_id=1, source_target_pairs={{0,8},{1,9},{2,10},{3,11},{4,12},{5,13},{6,14},{7,15},{8,0},{9,1},... | collective-permute-start | bytes 1105928 | tf_op jit(solution)/shard_map/ppermute | solution.py:57
  414.1 29.0 %collective-permute-start.58 = (bf16[256,768]{1,0:T(8,128)(2,1)S(1)}, bf16[256,768]{1,0:T(8,128)(2,1)S(1)}, u32[]{:S(2)}, u32[]{:S(2)}) collective-permute-start(bf16[256,768]{1,0:T(8,128)(2,1)S(1)} %get-tuple-element.368), channel_id=1, source_target_pairs={{1,0},{0,1},{5,2},{4,3},{3,4},{2,5},{7,6},{6,7},{9,8},{8,9},{13,10... | collective-permute-start | bytes 1179656 | tf_op jit(solution)/shard_map/ppermute | solution.py:568
  416.0 27.1 %collective-permute-start.59 = (bf16[256,768]{1,0:T(8,128)(2,1)S(1)}, bf16[256,768]{1,0:T(8,128)(2,1)S(1)}, u32[]{:S(2)}, u32[]{:S(2)}) collective-permute-start(bf16[256,768]{1,0:T(8,128)(2,1)S(1)} %get-tuple-element.367), channel_id=1, source_target_pairs={{0,0},{1,1},{4,2},{5,3},{2,4},{3,5},{6,6},{7,7},{8,8},{9,9},{12,10... | collective-permute-start | bytes 1179656 | tf_op jit(solution)/shard_map/ppermute | solution.py:568
  (178 other events, 1320.5 us)

commit v3 on v2

--- a/solution.py
+++ b/solution.py
@@ -563,8 +563,8 @@
     def to_groups(values):
         return jnp.concatenate([to_group(values, turn) for turn in range(seqs)], 0)
 
-    def from_groups(values):
-        got = [
+    def send_back(values):
+        return [
             lax.ppermute(
                 values[turn * width : (turn + 1) * width],
                 AXES,
@@ -572,6 +572,8 @@
             )
             for turn in range(seqs)
         ]
+
+    def put_back(got):
         return jnp.stack(
             [
                 functools.reduce(
@@ -712,7 +714,7 @@
     )
     target = to_groups(after(teacher, middle))
     result, second_saved = forward_layer(grid, group_bits, middle, params, mask)
-    layer_out = from_groups(result.astype(BF))
+    layer_got = send_back(result.astype(BF))
     diff = (result - target.astype(F32)) * live
     error = jnp.sum(diff * diff)
 
@@ -728,6 +730,8 @@
     a = Backward(grid, group_bits, first_saved, params, mask)
     a.top(d_middle)
     downs = grads(grid, [b.act_low, a.act_low], [b.d_down, a.d_down])
+    downs, layer_got = meet(downs, layer_got)
+    layer_out = put_back(layer_got)
     reduce_down, reduce_up, reduce_rest = Reduce(grid), Reduce(grid), Reduce(grid)
     reduce_down.add(*downs)
     a.d_down = after(a.d_down, downs)
@@ -775,7 +779,7 @@
     reduce_rest.add(pick(small, 1 - grid.core).astype(BF), pick(small, grid.core))
     a.d_query = after(a.d_query, rest_kv)
     d_start = a.start()
-    grad_tokens = from_groups(d_start.astype(BF))
+    grad_tokens = put_back(send_back(d_start.astype(BF)))
     reduce_rest.first(d_start)
     reduce_up.third(reduce_rest.sent())
     reduce_rest.second()

time: 477 us -> 474 us (level)
  waiting for transfers between devices: 87.3 us -> 79.7 us
    ppermute x4, waiting for transfers between devices: 7.93 us -> 0.01 us  [send_back(): lax.ppermute(values[turn * width:(turn + 1) * width], AXES, [(there, here...]
    unnamed x284 -> x288, local copies, waits for them, and re-layouts: 24.1 us -> 27.2 us
  transfers between devices with their start and end apart: 70 -> 70, of which waited for: 19 -> 18; matrix products, arithmetic and copies ran while one was open for 28% -> 30% of each run, Pallas kernels for 18% -> 20%
where the time goes in v3:
time: 474 us; the launch traced here: 466 us
  Pallas kernels  121 us (26%)
  waiting for transfers between devices  79.7 us (17%)
  matrix products  75.9 us (16%)
  local copies, waits for them, and re-layouts  63.9 us (13%)
  starting transfers between devices  59.5 us (13%)
  other arithmetic  55.6 us (12%)
  between operations  11 us (2%)
    ppermute x62, waiting for transfers between devices, flip(): return lax.ppermute(value, AXES, [(i, i ^ mask) for i in range(self.n)])  59.9 us
    ppermute x62, starting transfers between devices, flip(): return lax.ppermute(value, AXES, [(i, i ^ mask) for i in range(self.n)])  42.3 us
    dot_general x10, matrix products, mm_back(): lax.dot_general(left, right, (((1,), (1,)), ((), ())), preferred_element_...  41.3 us
    pallas_call x3, Pallas kernels, attend_back(): pl.pallas_call(functools.partial(attend_back_kernel, count, HD ** (-0.5))...  40.5 us
    pallas_call x5, Pallas kernels, grads(): pl.pallas_call(functools.partial(grads_kernel, count, top, whole), out_sh...  35.7 us
    dot_general x10, matrix products, mm(): return jnp.dot(left, right, preferred_element_type=F32)  34.6 us
    pallas_call x3, Pallas kernels, attend(): pl.pallas_call(kernel, grid=(pairs,), in_specs=[at(0), pl.BlockSpec((coun...  30.5 us
    unnamed x288, local copies, waits for them, and re-layouts  27.2 us
  transfers between devices with their start and end apart: 70, of which 18 were waited for; matrix products, arithmetic and copies ran while one was open for 30% of the time, Pallas kernels for 20%

profile of v3, /device:TPU:1, one launch (start us, length us, event | category | flops | bytes accessed | tf_op | source)
XLA Modules:
  0.0 466.4 jit_solution(3841465952089933721)
XLA Ops:
  17.6 8.3 %collective-permute-done.3 = bf16[48,128]{1,0:T(8,128)(2,1)S(1)} collective-permute-done((bf16[48,128]{1,0:T(8,128)(2,1)S(1)}, bf16[48,128]{1,0:T(8,128)(2,1)S(1)}, u32[]{:S(2)}, u32[]{:S(2)}) %collective-permute-start.3) | collective-permute-done | bytes 12320 | tf_op jit(solution)/shard_map/ppermute | solution.py:57
  34.0 11.6 %collective-permute-done.8 = bf16[256,768]{1,0:T(8,128)(2,1)S(1)} collective-permute-done((bf16[256,768]{1,0:T(8,128)(2,1)S(1)}, bf16[256,768]{1,0:T(8,128)(2,1)S(1)}, u32[]{:S(2)}, u32[]{:S(2)}) %collective-permute-start.8) | collective-permute-done | bytes 393248 | tf_op jit(solution)/shard_map/ppermute | solution.py:561
  53.2 5.5 %collective-permute-done.9.refs_3_ = bf16[96,1152]{1,0:T(8,128)(2,1)S(1)} collective-permute-done((bf16[96,1152]{1,0:T(8,128)(2,1)S(1)}, bf16[96,1152]{1,0:T(8,128)(2,1)S(1)}, u32[]{:S(2)}, u32[]{:S(2)}) %collective-permute-start.9) | collective-permute-done | bytes 221216 | tf_op jit(solution)/shard_map/ppermute | solution.py:57
  59.2 8.2 %collective-permute-done.12 = bf16[256,768]{1,0:T(8,128)(2,1)S(1)} collective-permute-done((bf16[256,768]{1,0:T(8,128)(2,1)S(1)}, bf16[256,768]{1,0:T(8,128)(2,1)S(1)}, u32[]{:S(2)}, u32[]{:S(2)}) %collective-permute-start.12) | collective-permute-done | bytes 393248 | tf_op jit(solution)/shard_map/ppermute | solution.py:561
  85.3 8.8 %collective-permute-done.21 = bf16[96,768]{1,0:T(8,128)(2,1)S(1)} collective-permute-done((bf16[96,768]{1,0:T(8,128)(2,1)S(1)}, bf16[96,768]{1,0:T(8,128)(2,1)S(1)}, u32[]{:S(2)}, u32[]{:S(2)}) %collective-permute-start.21) | collective-permute-done | bytes 147488 | tf_op jit(solution)/shard_map/ppermute | solution.py:57
  97.0 8.3 %attend.3 = (bf16[512,768]{1,0:T(8,128)(2,1)}, f32[6,8,512]{2,1,0:T(8,128)}) custom-call(bf16[512,768]{1,0:T(8,128)(2,1)} %add_convert_fusion.4.refs_0_.q_ref, bf16[2,512,128]{2,1,0:T(8,128)(2,1)} %select_convert_fusion.refs_1_.mask_ref, bf16[512,1536]{1,0:T(8,128)(2,1)} %copy-done, bf16[512,1536]{1,0:T(8,128)(2,1)} %copy-done.1, bf16[512,1536]{1,0:T(8,128)(2,1)} %copy-done, ...), custom_call_target="tpu_custom_call" | custom-call | tf_op jit(solution)/shard_map/attend/pallas_call | solution.py:332
  109.4 8.1 %attend.4 = (bf16[512,768]{1,0:T(8,128)(2,1)}, f32[6,8,512]{2,1,0:T(8,128)}) custom-call(bf16[512,768]{1,0:T(8,128)(2,1)} %add_convert_fusion.4.refs_0_.q_ref, bf16[2,512,128]{2,1,0:T(8,128)(2,1)} %select_convert_fusion.refs_1_.mask_ref, bf16[512,1536]{1,0:T(8,128)(2,1)} %copy-done, ...), custom_call_target="tpu_custom_call", output_to_operand_aliasing={{0}: (6, {}), {1}: (7, {})} | custom-call | tf_op jit(solution)/shard_map/attend/pallas_call | solution.py:332
  125.8 5.4 %assemble.4 = (bf16[768,768]{1,0:T(8,128)(2,1)}, bf16[768,3072]{1,0:T(8,128)(2,1)}) custom-call(s32[1]{0:T(128)} %bitcast.12.me, bf16[96,3840]{1,0:T(8,128)(2,1)} %copy-done.42, bf16[96,3840]{1,0:T(8,128)(2,1)} %copy-done.19, bf16[96,3840]{1,0:T(8,128)(2,1)} %copy-done.20, bf16[96,1920]{1,0:T(8,128)(2,1)} %copy-done.62, bf16[96,1920]{1,0:T(8,128)(2,1)} %copy-done.63, ...), custom_call_target="tpu_custom_call" | custom-call | tf_op jit(solution)/shard_map/assemble/pallas_call | solution.py:152
  142.0 9.0 %multiply_convert_fusion.1 = (bf16[512,3072]{1,0:T(8,128)(2,1)}, f32[512,3072]{1,0:T(8,128)}) fusion(f32[3072]{0:T(1024)S(1)} %add.597, bf16[512,768]{1,0:T(8,128)(2,1)S(1)} %fusion.16.refs_1_, bf16[768,3072]{1,0:T(8,128)(2,1)} %get-tuple-element.187), kind=kOutput, calls=%fused_computation.21 | convolution fusion | flops 2431647744 | bytes 14954496 | tf_op jit(solution)/shard_map/dot_general | solution.py:21
  159.6 6.0 %fusion.65 = (f32[512]{0:T(512)S(1)}, f32[512,768]{1,0:T(8,128)S(1)}) fusion(f32[768]{0:T(1024)S(1)} %copy-done.106, bf16[512,3072]{1,0:T(8,128)(2,1)} %get-tuple-element.191.refs_1_, bf16[3072,768]{1,0:T(8,128)(2,1)} %assemble.5, f32[768]{0:T(1024)S(1)} %get-tuple-element.320, f32[768]{0:T(1024)S(1)} %get-tuple-element.321, f32[512]{0:T(512)S(1)} %fusion.37, ...), kind=kOutput, calls=%fused_computation.298 | convolution fusion | flops 2418671104 | bytes 11025408 | tf_op jit(solution)/shard_map/dot_general | solution.py:21
  178.3 14.1 %attend.5 = (bf16[512,768]{1,0:T(8,128)(2,1)}, f32[6,8,512]{2,1,0:T(8,128)}) custom-call(bf16[512,768]{1,0:T(8,128)(2,1)} %add_convert_fusion.3.refs_0_.q_ref, bf16[2,512,128]{2,1,0:T(8,128)(2,1)} %select_convert_fusion.refs_1_.mask_ref, bf16[512,1536]{1,0:T(8,128)(2,1)} %copy-done.2, bf16[512,1536]{1,0:T(8,128)(2,1)} %copy-done.3, ...), custom_call_target="tpu_custom_call" | custom-call | tf_op jit(solution)/shard_map/attend/pallas_call | solution.py:332
  195.5 6.1 %multiply_convert_fusion = (bf16[512,3072]{1,0:T(8,128)(2,1)S(1)}, f32[512,3072]{1,0:T(8,128)S(1)}) fusion(f32[3072]{0:T(1024)S(1)} %add.597, bf16[512,768]{1,0:T(8,128)(2,1)S(1)} %fusion.17.refs_0_, bf16[768,3072]{1,0:T(8,128)(2,1)} %get-tuple-element.187), kind=kOutput, calls=%fused_computation.20 | convolution fusion | flops 2431647744 | bytes 14954496 | tf_op jit(solution)/shard_map/dot_general | solution.py:21
  208.4 7.2 %convert_reduce_fusion.1 = (f32[3072]{0:T(1024)}, bf16[512,3072]{1,0:T(8,128)(2,1)S(1)}) fusion(f32[512,3072]{1,0:T(8,128)S(1)} %get-tuple-element.433, f32[3072]{0:T(1024)S(1)} %add.597, bf16[512,768]{1,0:T(8,128)(2,1)S(1)} %get-tuple-element.340.refs_2_, bf16[3072,768]{1,0:T(8,128)(2,1)S(1)} %bitcast.176), kind=kOutput, calls=%fused_computation.19 | convolution fusion | flops 2452091904 | bytes 14966784 | tf_op jit(solution)/shard_map/dot_general | solution.py:29
  223.7 19.0 %attend_back.3 = (bf16[512,768]{1,0:T(8,128)(2,1)}, bf16[2,512,768]{2,1,0:T(8,128)(2,1)}, bf16[2,512,768]{2,1,0:T(8,128)(2,1)}) custom-call(bf16[512,768]{1,0:T(8,128)(2,1)} %add_convert_fusion.3.refs_0_.q_ref, bf16[512,768]{1,0:T(8,128)(2,1)} %convolution_convert_fusion.1.do_ref, bf16[512,768]{1,0:T(8,128)(2,1)} %get-tuple-element.198.o_ref.refs_0_, ...), custom_call_target="tpu_custom_call" | custom-call | tf_op jit(solution)/shard_map/attend_back/pallas_call | solution.py:397
  270.0 9.8 %grads.5 = (bf16[4,384,768]{2,1,0:T(8,128)(2,1)}, f32[4,384,768]{2,1,0:T(8,128)}) custom-call(s32[1]{0:T(128)} %bitcast.core, bf16[512,3072]{1,0:T(8,128)(2,1)} %copy-done.30, bf16[512,3072]{1,0:T(8,128)(2,1)} %get-tuple-element.191.refs_1_, bf16[512,768]{1,0:T(8,128)(2,1)} %copy-done.40, bf16[512,768]{1,0:T(8,128)(2,1)} %add_convert_fusion.6.refs_3_), custom_call_target="tpu_custom_call" | custom-call | tf_op jit(solution)/shard_map/grads/pallas_call | solution.py:197
  279.9 9.9 %fusion.6.refs_3_ = bf16[512,3072]{1,0:T(8,128)(2,1)} fusion(f32[512,3072]{1,0:T(8,128)} %get-tuple-element.427, f32[3072]{0:T(1024)S(1)} %copy-done.94, bf16[512,768]{1,0:T(8,128)(2,1)S(1)} %copy-done.9, bf16[3072,768]{1,0:T(8,128)(2,1)} %assemble.5), kind=kOutput, calls=%fused_computation.10 | convolution fusion | flops 2448949248 | bytes 14954496 | tf_op jit(solution)/shard_map/dot_general | solution.py:29
  289.9 10.3 %grads.6 = (bf16[4,96,3072]{2,1,0:T(8,128)(2,1)}, f32[4,96,3072]{2,1,0:T(8,128)}) custom-call(s32[1]{0:T(128)} %bitcast.core, bf16[512,768]{1,0:T(8,128)(2,1)} %copy-done.39, bf16[512,768]{1,0:T(8,128)(2,1)} %copy-done.38, bf16[512,3072]{1,0:T(8,128)(2,1)} %copy-done.31, bf16[512,3072]{1,0:T(8,128)(2,1)} %fusion.6.refs_3_), custom_call_target="tpu_custom_call" | custom-call | tf_op jit(solution)/shard_map/grads/pallas_call | solution.py:197
  300.7 6.5 %multiply_reduce_fusion.2 = (f32[768]{0:T(1024)}, f32[512]{0:T(512)S(1)}, f32[768]{0:T(1024)}, f32[512,768]{1,0:T(8,128)S(1)}) fusion(f32[512,768]{1,0:T(8,128)S(1)} %get-tuple-element.357, f32[512]{0:T(512)S(1)} %copy-done.84, f32[512]{0:T(512)S(1)} %copy-done.78, f32[768]{0:T(1024)S(1)} %get-tuple-element.321, bf16[512,3072]{1,0:T(8,128)(2,1)S(1)} %copy-done.4, ...), kind=kOutput, calls=%fused_computation.42 | convolution fusion | flops 2419849216 | bytes 12600320 | tf_op jit(solution)/shard_map/dot_general | solution.py:29
  333.6 10.8 %attend_back.4 = (bf16[512,384]{1,0:T(8,128)(2,1)}, bf16[2,512,384]{2,1,0:T(8,128)(2,1)}, bf16[2,512,384]{2,1,0:T(8,128)(2,1)}) custom-call(bf16[512,768]{1,0:T(8,128)(2,1)} %add_convert_fusion.4.refs_0_.q_ref, bf16[512,768]{1,0:T(8,128)(2,1)} %convolution_convert_fusion.do_ref, bf16[512,768]{1,0:T(8,128)(2,1)} %get-tuple-element.175.refs_1_.o_ref, ...), custom_call_target="tpu_custom_call" | custom-call | tf_op jit(solution)/shard_map/attend_back/pallas_call | solution.py:397
  360.2 10.6 %attend_back.5 = (bf16[512,384]{1,0:T(8,128)(2,1)}, bf16[2,512,384]{2,1,0:T(8,128)(2,1)}, bf16[2,512,384]{2,1,0:T(8,128)(2,1)}) custom-call(bf16[512,768]{1,0:T(8,128)(2,1)} %add_convert_fusion.4.refs_0_.q_ref, bf16[512,768]{1,0:T(8,128)(2,1)} %convolution_convert_fusion.do_ref, bf16[512,768]{1,0:T(8,128)(2,1)} %get-tuple-element.175.refs_1_.o_ref, ...), custom_call_target="tpu_custom_call" | custom-call | tf_op jit(solution)/shard_map/attend_back/pallas_call | solution.py:397
  389.8 6.5 %grads.9 = (bf16[4,96,1536]{2,1,0:T(8,128)(2,1)}, f32[4,96,1536]{2,1,0:T(8,128)}) custom-call(s32[1]{0:T(128)} %bitcast.core, bf16[512,768]{1,0:T(8,128)(2,1)} %copy-done.8, bf16[512,768]{1,0:T(8,128)(2,1)} %copy-done.15, bf16[512,1536]{1,0:T(8,128)(2,1)} %pad_maximum_fusion.2.refs_2_, bf16[512,1536]{1,0:T(8,128)(2,1)} %pad_maximum_fusion.3.refs_3_), custom_call_target="tpu_custom_call" | custom-call | tf_op jit(solution)/shard_map/grads/pallas_call | solution.py:197
  424.2 5.5 %collective-permute-done.53 = bf16[2,96,1280]{2,1,0:T(8,128)(2,1)S(1)} collective-permute-done((bf16[2,96,1280]{2,1,0:T(8,128)(2,1)S(1)}, bf16[2,96,1280]{2,1,0:T(8,128)(2,1)S(1)}, u32[]{:S(2)}, u32[]{:S(2)}) %collective-permute-start.53) | collective-permute-done | bytes 491552 | tf_op jit(solution)/shard_map/ppermute | solution.py:57
  446.2 5.2 %collective-permute-done.56 = bf16[2,24,2560]{2,1,0:T(8,128)(2,1)S(1)} collective-permute-done((bf16[2,24,2560]{2,1,0:T(8,128)(2,1)S(1)}, bf16[2,24,2560]{2,1,0:T(8,128)(2,1)S(1)}, u32[]{:S(2)}, u32[]{:S(2)}) %collective-permute-start.56) | collective-permute-done | bytes 245792 | tf_op jit(solution)/shard_map/ppermute | solution.py:57
  453.0 6.3 %collective-permute-done.57 = bf16[1,24,2560]{2,1,0:T(8,128)(2,1)S(1)} collective-permute-done((bf16[1,24,2560]{2,1,0:T(8,128)(2,1)S(1)}, bf16[1,24,2560]{2,1,0:T(8,128)(2,1)S(1)}, u32[]{:S(2)}, u32[]{:S(2)}) %collective-permute-start.57) | collective-permute-done | bytes 122912 | tf_op jit(solution)/shard_map/ppermute | solution.py:57
  (631 shorter events, 248.2 us)
Async XLA Ops:
  7.9 42.7 %collective-permute-start.16 = (s32[2]{0:T(128)}, s32[2]{0:T(128)S(1)}, u32[]{:S(2)}, u32[]{:S(2)}) collective-permute-start(s32[2]{0:T(128)} %param.19), channel_id=1, source_target_pairs={{0,4},{1,5},{2,6},{3,7},{4,0},{5,1},{6,2},{7,3},{8,12},{9,13},{10,... | collective-permute-start | bytes 32 | tf_op jit(solution)/shard_map/ppermute | solution.py:57
  47.5 19.9 %collective-permute-start.11 = (bf16[192,2432]{1,0:T(8,128)(2,1)}, bf16[192,2432]{1,0:T(8,128)(2,1)}, u32[]{:S(2)}, u32[]{:S(2)}) collective-permute-start(bf16[192,2432]{1,0:T(8,128)(2,1)} %pad_maximum_fusion.9), channel_id=1, source_target_pairs={{0,4},{1,5},{2,6},{3,7},{4,0},{5,1},{6,2},{7,3},{8,12},{9,13},{10,... | collective-permute-start | bytes 2801672 | tf_op jit(solution)/shard_map/ppermute | solution.py:57
  82.8 22.4 %collective-permute-start.18 = (bf16[96,3840]{1,0:T(8,128)(2,1)S(1)}, bf16[96,3840]{1,0:T(8,128)(2,1)S(1)}, u32[]{:S(2)}, u32[]{:S(2)}) collective-permute-start(bf16[96,3840]{1,0:T(8,128)(2,1)S(1)} %pad_maximum_fusion.12.refs_0_), channel_id=1, source_target_pairs={{0,8},{1,9},{2,10},{3,11},{4,12},{5,13},{6,14},{7,15},{8,0},{9,1},... | collective-permute-start | bytes 2211848 | tf_op jit(solution)/shard_map/ppermute | solution.py:57
  83.2 22.1 %collective-permute-start.19 = (bf16[96,3840]{1,0:T(8,128)(2,1)S(1)}, bf16[96,3840]{1,0:T(8,128)(2,1)S(1)}, u32[]{:S(2)}, u32[]{:S(2)}) collective-permute-start(bf16[96,3840]{1,0:T(8,128)(2,1)S(1)} %pad_maximum_fusion.12.refs_0_), channel_id=1, source_target_pairs={{0,16},{1,17},{2,18},{3,19},{4,20},{5,21},{6,22},{7,23},{8,24},{9,... | collective-permute-start | bytes 2211848 | tf_op jit(solution)/shard_map/ppermute | solution.py:57
  83.4 21.9 %collective-permute-start.20 = (bf16[96,3840]{1,0:T(8,128)(2,1)S(1)}, bf16[96,3840]{1,0:T(8,128)(2,1)S(1)}, u32[]{:S(2)}, u32[]{:S(2)}) collective-permute-start(bf16[96,3840]{1,0:T(8,128)(2,1)S(1)} %pad_maximum_fusion.12.refs_0_), channel_id=1, source_target_pairs={{0,4},{1,5},{2,6},{3,7},{4,0},{5,1},{6,2},{7,3},{8,12},{9,13},{10,... | collective-permute-start | bytes 2211848 | tf_op jit(solution)/shard_map/ppermute | solution.py:57
  170.5 34.3 %collective-permute-start.37 = (bf16[256,768]{1,0:T(8,128)(2,1)S(1)}, bf16[256,768]{1,0:T(8,128)(2,1)S(1)}, u32[]{:S(2)}, u32[]{:S(2)}) collective-permute-start(bf16[256,768]{1,0:T(8,128)(2,1)S(1)} %get-tuple-element.385), channel_id=1, source_target_pairs={{0,0},{1,1},{2,4},{3,5},{4,2},{5,3},{6,6},{7,7},{8,8},{9,9},{10,12... | collective-permute-start | bytes 1179656 | tf_op jit(solution)/shard_map/ppermute | solution.py:561
  173.3 31.6 %collective-permute-start.38 = (bf16[256,768]{1,0:T(8,128)(2,1)S(1)}, bf16[256,768]{1,0:T(8,128)(2,1)S(1)}, u32[]{:S(2)}, u32[]{:S(2)}) collective-permute-start(bf16[256,768]{1,0:T(8,128)(2,1)S(1)} %get-tuple-element.386), channel_id=1, source_target_pairs={{0,1},{1,0},{2,5},{3,4},{4,3},{5,2},{6,7},{7,6},{8,9},{9,8},{10,13... | collective-permute-start | bytes 1179656 | tf_op jit(solution)/shard_map/ppermute | solution.py:561
  242.7 19.1 %collective-permute-start.39 = (bf16[2,512,768]{2,1,0:T(8,128)(2,1)}, bf16[2,512,768]{2,1,0:T(8,128)(2,1)}, u32[]{:S(2)}, u32[]{:S(2)}) collective-permute-start(bf16[2,512,768]{2,1,0:T(8,128)(2,1)} %get-tuple-element.203), channel_id=1, source_target_pairs={{0,4},{1,5},{2,6},{3,7},{4,0},{5,1},{6,2},{7,3},{8,12},{9,13},{10,... | collective-permute-start | bytes 4718600 | tf_op jit(solution)/shard_map/ppermute | solution.py:57
  248.8 31.0 %collective-permute-start.40 = (bf16[256,768]{1,0:T(8,128)(2,1)}, bf16[256,768]{1,0:T(8,128)(2,1)S(1)}, u32[]{:S(2)}, u32[]{:S(2)}) collective-permute-start(bf16[256,768]{1,0:T(8,128)(2,1)} %get-tuple-element.384), channel_id=1, source_target_pairs={{0,0},{1,1},{4,2},{5,3},{2,4},{3,5},{6,6},{7,7},{8,8},{9,9},{12,10... | collective-permute-start | bytes 1179656 | tf_op jit(solution)/shard_map/ppermute | solution.py:568
  251.0 28.9 %collective-permute-start.41 = (bf16[256,768]{1,0:T(8,128)(2,1)}, bf16[256,768]{1,0:T(8,128)(2,1)}, u32[]{:S(2)}, u32[]{:S(2)}) collective-permute-start(bf16[256,768]{1,0:T(8,128)(2,1)} %get-tuple-element.383), channel_id=1, source_target_pairs={{1,0},{0,1},{5,2},{4,3},{3,4},{2,5},{7,6},{6,7},{9,8},{8,9},{13,10... | collective-permute-start | bytes 1179656 | tf_op jit(solution)/shard_map/ppermute | solution.py:568
  279.8 45.3 %collective-permute-start.42 = (bf16[4,384,768]{2,1,0:T(8,128)(2,1)}, bf16[4,384,768]{2,1,0:T(8,128)(2,1)}, u32[]{:S(2)}, u32[]{:S(2)}) collective-permute-start(bf16[4,384,768]{2,1,0:T(8,128)(2,1)} %get-tuple-element.208), channel_id=1, source_target_pairs={{0,4},{1,5},{2,6},{3,7},{4,0},{5,1},{6,2},{7,3},{8,12},{9,13},{10,... | collective-permute-start | bytes 7077896 | tf_op jit(solution)/shard_map/ppermute | solution.py:57
  300.2 44.2 %collective-permute-start.46 = (bf16[4,96,3072]{2,1,0:T(8,128)(2,1)}, bf16[4,96,3072]{2,1,0:T(8,128)(2,1)}, u32[]{:S(2)}, u32[]{:S(2)}) collective-permute-start(bf16[4,96,3072]{2,1,0:T(8,128)(2,1)} %get-tuple-element.211), channel_id=1, source_target_pairs={{0,4},{1,5},{2,6},{3,7},{4,0},{5,1},{6,2},{7,3},{8,12},{9,13},{10,... | collective-permute-start | bytes 7077896 | tf_op jit(solution)/shard_map/ppermute | solution.py:57
  314.7 29.7 %collective-permute-start.47 = (bf16[4,96,768]{2,1,0:T(8,128)(2,1)}, bf16[4,96,768]{2,1,0:T(8,128)(2,1)}, u32[]{:S(2)}, u32[]{:S(2)}) collective-permute-start(bf16[4,96,768]{2,1,0:T(8,128)(2,1)} %get-tuple-element.214), channel_id=1, source_target_pairs={{0,4},{1,5},{2,6},{3,7},{4,0},{5,1},{6,2},{7,3},{8,12},{9,13},{10,... | collective-permute-start | bytes 1769480 | tf_op jit(solution)/shard_map/ppermute | solution.py:57
  330.0 25.4 %collective-permute-start.45 = (bf16[2,384,384]{2,1,0:T(8,128)(2,1)}, bf16[2,384,384]{2,1,0:T(8,128)(2,1)}, u32[]{:S(2)}, u32[]{:S(2)}) collective-permute-start(bf16[2,384,384]{2,1,0:T(8,128)(2,1)} %fusion.22), channel_id=1, source_target_pairs={{0,16},{1,17},{2,18},{3,19},{4,20},{5,21},{6,22},{7,23},{8,24},{9,... | collective-permute-start | bytes 1769480 | tf_op jit(solution)/shard_map/ppermute | solution.py:57
  331.3 24.2 %collective-permute-start.44 = (bf16[2,384,384]{2,1,0:T(8,128)(2,1)}, bf16[2,384,384]{2,1,0:T(8,128)(2,1)}, u32[]{:S(2)}, u32[]{:S(2)}) collective-permute-start(bf16[2,384,384]{2,1,0:T(8,128)(2,1)} %fusion.21), channel_id=1, source_target_pairs={{0,8},{1,9},{2,10},{3,11},{4,12},{5,13},{6,14},{7,15},{8,0},{9,1},... | collective-permute-start | bytes 1769480 | tf_op jit(solution)/shard_map/ppermute | solution.py:57
  351.5 27.0 %collective-permute-start.61 = (bf16[2,96,1920]{2,1,0:T(8,128)(2,1)}, bf16[2,96,1920]{2,1,0:T(8,128)(2,1)}, u32[]{:S(2)}, u32[]{:S(2)}) collective-permute-start(bf16[2,96,1920]{2,1,0:T(8,128)(2,1)} %fusion.20), channel_id=1, source_target_pairs={{0,16},{1,17},{2,18},{3,19},{4,20},{5,21},{6,22},{7,23},{8,24},{9,... | collective-permute-start | bytes 2211848 | tf_op jit(solution)/shard_map/ppermute | solution.py:57
  353.7 24.8 %collective-permute-start.60 = (bf16[2,96,1920]{2,1,0:T(8,128)(2,1)}, bf16[2,96,1920]{2,1,0:T(8,128)(2,1)}, u32[]{:S(2)}, u32[]{:S(2)}) collective-permute-start(bf16[2,96,1920]{2,1,0:T(8,128)(2,1)} %fusion.19), channel_id=1, source_target_pairs={{0,8},{1,9},{2,10},{3,11},{4,12},{5,13},{6,14},{7,15},{8,0},{9,1},... | collective-permute-start | bytes 2211848 | tf_op jit(solution)/shard_map/ppermute | solution.py:57
  359.1 25.7 %collective-permute-start.66 = (bf16[384,384]{1,0:T(8,128)(2,1)}, bf16[384,384]{1,0:T(8,128)(2,1)S(1)}, u32[]{:S(2)}, u32[]{:S(2)}) collective-permute-start(bf16[384,384]{1,0:T(8,128)(2,1)} %get-tuple-element.443), channel_id=1, source_target_pairs={{0,16},{1,17},{2,18},{3,19},{4,20},{5,21},{6,22},{7,23},{8,24},{9,... | collective-permute-start | bytes 884744 | tf_op jit(solution)/shard_map/ppermute | solution.py:57
  359.5 26.3 %collective-permute-start.67 = (bf16[384,384]{1,0:T(8,128)(2,1)S(1)}, bf16[384,384]{1,0:T(8,128)(2,1)}, u32[]{:S(2)}, u32[]{:S(2)}) collective-permute-start(bf16[384,384]{1,0:T(8,128)(2,1)S(1)} %get-tuple-element.444), channel_id=1, source_target_pairs={{0,8},{1,9},{2,10},{3,11},{4,12},{5,13},{6,14},{7,15},{8,0},{9,1},... | collective-permute-start | bytes 884744 | tf_op jit(solution)/shard_map/ppermute | solution.py:57
  377.3 33.5 %collective-permute-start.48 = (bf16[4,96,768]{2,1,0:T(8,128)(2,1)}, bf16[4,96,768]{2,1,0:T(8,128)(2,1)}, u32[]{:S(2)}, u32[]{:S(2)}) collective-permute-start(bf16[4,96,768]{2,1,0:T(8,128)(2,1)} %get-tuple-element.229), channel_id=1, source_target_pairs={{0,4},{1,5},{2,6},{3,7},{4,0},{5,1},{6,2},{7,3},{8,12},{9,13},{10,... | collective-permute-start | bytes 1769480 | tf_op jit(solution)/shard_map/ppermute | solution.py:57
  382.7 36.8 %collective-permute-start.62 = (bf16[96,1920]{1,0:T(8,128)(2,1)}, bf16[96,1920]{1,0:T(8,128)(2,1)}, u32[]{:S(2)}, u32[]{:S(2)}) collective-permute-start(bf16[96,1920]{1,0:T(8,128)(2,1)} %fusion.25), channel_id=1, source_target_pairs={{0,16},{1,17},{2,18},{3,19},{4,20},{5,21},{6,22},{7,23},{8,24},{9,... | collective-permute-start | bytes 1105928 | tf_op jit(solution)/shard_map/ppermute | solution.py:57
  384.9 36.0 %collective-permute-start.63 = (bf16[96,1920]{1,0:T(8,128)(2,1)}, bf16[96,1920]{1,0:T(8,128)(2,1)}, u32[]{:S(2)}, u32[]{:S(2)}) collective-permute-start(bf16[96,1920]{1,0:T(8,128)(2,1)} %fusion.26), channel_id=1, source_target_pairs={{0,8},{1,9},{2,10},{3,11},{4,12},{5,13},{6,14},{7,15},{8,0},{9,1},... | collective-permute-start | bytes 1105928 | tf_op jit(solution)/shard_map/ppermute | solution.py:57
  410.8 29.0 %collective-permute-start.58 = (bf16[256,768]{1,0:T(8,128)(2,1)S(1)}, bf16[256,768]{1,0:T(8,128)(2,1)S(1)}, u32[]{:S(2)}, u32[]{:S(2)}) collective-permute-start(bf16[256,768]{1,0:T(8,128)(2,1)S(1)} %get-tuple-element.376), channel_id=1, source_target_pairs={{1,0},{0,1},{5,2},{4,3},{3,4},{2,5},{7,6},{6,7},{9,8},{8,9},{13,10... | collective-permute-start | bytes 1179656 | tf_op jit(solution)/shard_map/ppermute | solution.py:568
  412.7 27.1 %collective-permute-start.59 = (bf16[256,768]{1,0:T(8,128)(2,1)S(1)}, bf16[256,768]{1,0:T(8,128)(2,1)S(1)}, u32[]{:S(2)}, u32[]{:S(2)}) collective-permute-start(bf16[256,768]{1,0:T(8,128)(2,1)S(1)} %get-tuple-element.375), channel_id=1, source_target_pairs={{0,0},{1,1},{4,2},{5,3},{2,4},{3,5},{6,6},{7,7},{8,8},{9,9},{12,10... | collective-permute-start | bytes 1179656 | tf_op jit(solution)/shard_map/ppermute | solution.py:568
  (180 other events, 1343.5 us)
